TPU v7x, 512 devices: a whole 4x4x16 slice. The times are simulated.
512 devices in a mesh: lon: 32 (over x, z_lo), lat: 16 (over y, z_hi, core).
Axes of the slice: x: 4, y: 4, z: 16 (z_hi: 2, z_lo: 8; z = z_hi * 8 + z_lo), core: 2. Of those that a mesh axis runs over, the one named last changes fastest.
Arguments:
- increment: bfloat16 [2, 127, 128, 4096], P(None, None, 'lat', 'lon'), may hold values from -6 to 6
- std_dev: bfloat16 [2, 127, 128, 4096], P(None, None, 'lat', 'lon'), may hold values from 0.5 to 4
- level_group: int32 [127], replicated, may hold values from 0 to 3, never falling along the last dimension, each value on 1 to 40 neighbouring positions
- lon_reach: float32 [2, 4, 4], replicated, may hold values from 8 to 16384
- lon_weight: float32 [2, 4, 4], replicated, may hold values from 0.2 to 1
- lat_reach: float32 [2, 4, 4], replicated, may hold values from 2 to 512
- lat_weight: float32 [2, 4, 4], replicated, may hold values from 0.2 to 1
- vertical: float32 [2, 127, 127], replicated, may hold values from -0.5 to 0.5
Outputs:
- covaried: bfloat16 [2, 127, 128, 4096], P(None, None, 'lat', 'lon')
Inputs may be any that keep to these rules, and one draw needn't show every extreme that they name: level_group never falls along the levels; each of the 4 groups holds 1 to 40 consecutive levels and one holds exactly 40.
All inputs are finite; a program needn't handle non-finite values.
Results may differ from a plain program's by a relative error of at most 0.003.
Values sent between devices are 32-bit elements; how exact they have to be, the bound alone decides.
A program may use at most 64 MiB of HBM per device.

v0:
```python
import jax
import jax.numpy as jnp
from jax import lax
from jax.sharding import PartitionSpec as P

MOST = 40


def prefix_2(part, axis, combine, identity, reverse):
    count = lax.axis_size(axis)
    place = lax.axis_index(axis)
    ahead = count - 1 - place if reverse else place
    gathered = jax.tree.map(lambda a: lax.all_gather(a, axis), part)
    state = jax.tree.map(lambda a, e: jnp.zeros_like(a) + jnp.asarray(e, a.dtype), part, identity)

    def one(step, state):
        source = count - 1 - step if reverse else step
        return combine(
            state, jax.tree.map(lambda a: lax.dynamic_index_in_dim(a, source, 0, False), gathered)
        )

    return lax.fori_loop(0, ahead, one, state)


def from_root(value, axis, source):
    kept = jnp.where(lax.axis_index(axis) == source, value, 0).astype(value.dtype)
    return lax.psum(kept, axis)


def level_values(onehot, grouped):
    return jnp.einsum("kg,vgp->vkp", onehot, grouped, precision=lax.Precision.HIGHEST)


def toeplitz_tables(inverse_group, weights_group, length):
    indices = jnp.arange(length)
    spacing = (indices[None, :] - indices[:, None]).astype(jnp.float32)
    rates = jnp.exp(-jnp.maximum(spacing, 0.0) * inverse_group[..., None, None])
    terms = jnp.sum(weights_group[..., None, None] * rates, axis=2)
    return jnp.where(spacing >= 0.0, terms, 0.0)


def grouped_product(current, blocks, level_group, pattern):
    levels = current.shape[1]
    result = jnp.zeros_like(current)
    for group in range(blocks.shape[1]):
        first_level = jnp.minimum(jnp.sum((level_group < group).astype(jnp.int32)), levels - MOST)
        window = lax.dynamic_slice_in_dim(current, first_level, MOST, 1)
        product = jnp.einsum(pattern, window, blocks[:, group], precision=lax.Precision.HIGHEST)
        labels = lax.dynamic_slice_in_dim(level_group, first_level, MOST, 0)
        member_mask = (labels == group)[None, :, None, None]
        previous = lax.dynamic_slice_in_dim(result, first_level, MOST, 1)
        result = lax.dynamic_update_slice_in_dim(
            result, previous + jnp.where(member_mask, product, 0.0), first_level, 1
        )
    return result


def affine_join(earlier, later):
    return (earlier[0] * later[0], later[0] * earlier[1] + later[1])


def cycle_carry(edge_sums, inverse_level, length, reverse):
    members = lax.axis_size("lon")
    inverse = jnp.transpose(inverse_level, (2, 0, 1))[..., None]
    closure = 1.0 - jnp.exp(-(members * length) * inverse)
    stride = jnp.exp(-length * inverse)
    factor, prefix = prefix_2(
        (stride, edge_sums),
        "lon",
        affine_join,
        (jnp.ones_like(stride), jnp.zeros_like(edge_sums)),
        reverse,
    )
    leaving = stride * prefix + edge_sums
    anchor = 0 if reverse else members - 1
    beside_all = from_root(leaving, "lon", anchor)
    return prefix + factor * beside_all / closure


def band_carry(edge_sums, inverse_level, length, reverse):
    inverse = jnp.transpose(inverse_level, (2, 0, 1))[..., None]
    stride = jnp.exp(-length * inverse)
    factor, prefix = prefix_2(
        (stride, edge_sums),
        "lat",
        affine_join,
        (jnp.ones_like(stride), jnp.zeros_like(edge_sums)),
        reverse,
    )
    return prefix


def lon_pass(current, blocks, inverse, weights, level_group, reverse):
    cells = current.shape[3]
    position = jnp.arange(cells).astype(jnp.float32)
    if reverse:
        edge_gap = position
        inward = cells - position
        pattern = "vkaj,vij->vkai"
    else:
        edge_gap = cells - 1.0 - position
        inward = position + 1.0
        pattern = "vkaj,vji->vkai"
    edge_weight = jnp.exp(-edge_gap * inverse[..., None])
    edge_sums = jnp.einsum("vkal,vkpl->pvka", current, edge_weight, precision=lax.Precision.HIGHEST)
    inside = grouped_product(current, blocks, level_group, pattern)
    incoming = cycle_carry(edge_sums, inverse, cells, reverse)
    decay = weights[..., None] * jnp.exp(-inward * inverse[..., None])
    return inside + jnp.einsum("pvka,vkpl->vkal", incoming, decay, precision=lax.Precision.HIGHEST)


def lat_pass(current, blocks, inverse, weights, level_group, reverse):
    height = current.shape[2]
    position = jnp.arange(height).astype(jnp.float32)
    if reverse:
        edge_gap = position
        inward = height - position
        pattern = "vkjl,vij->vkil"
    else:
        edge_gap = height - 1.0 - position
        inward = position + 1.0
        pattern = "vkjl,vji->vkil"
    edge_weight = jnp.exp(-edge_gap * inverse[..., None])
    edge_sums = jnp.einsum("vkal,vkpa->pvkl", current, edge_weight, precision=lax.Precision.HIGHEST)
    inside = grouped_product(current, blocks, level_group, pattern)
    incoming = band_carry(edge_sums, inverse, height, reverse)
    decay = weights[..., None] * jnp.exp(-inward * inverse[..., None])
    return inside + jnp.einsum("pvkl,vkpa->vkal", incoming, decay, precision=lax.Precision.HIGHEST)


def per_device(
    increment, std_dev, level_group, lon_reach, lon_weight, lat_reach, lat_weight, vertical
):
    height = increment.shape[2]
    cells = increment.shape[3]
    groups = lon_reach.shape[1]
    onehot = (level_group[:, None] == jnp.arange(groups, dtype=jnp.int32)[None, :]).astype(
        jnp.float32
    )
    inverse_lon_group = 1.0 / lon_reach
    weights_lon_group = lon_weight * (1.0 - jnp.exp(-inverse_lon_group))
    inverse_lat_group = 1.0 / lat_reach
    weights_lat_group = lat_weight * (1.0 - jnp.exp(-inverse_lat_group))
    inverse_lon = level_values(onehot, inverse_lon_group)
    inverse_lat = level_values(onehot, inverse_lat_group)
    weights_lat = level_values(onehot, weights_lat_group)
    blocks_lat = toeplitz_tables(inverse_lat_group, weights_lat_group, height)
    spread_dev = std_dev.astype(jnp.float32)
    current = spread_dev * increment.astype(jnp.float32)
    weights_lon = level_values(onehot, weights_lon_group)
    blocks_lon = toeplitz_tables(inverse_lon_group, weights_lon_group, cells)
    current = lon_pass(current, blocks_lon, inverse_lon, weights_lon, level_group, False)
    current = lon_pass(current, blocks_lon, inverse_lon, weights_lon, level_group, True)
    current = lat_pass(current, blocks_lat, inverse_lat, weights_lat, level_group, False)
    current = lat_pass(current, blocks_lat, inverse_lat, weights_lat, level_group, True)
    mixed = jnp.einsum("vkj,vjal->vkal", vertical, current, precision=lax.Precision.HIGHEST)
    return (spread_dev * mixed).astype(jnp.bfloat16)


def solution(mesh):
    placed = (
        P(None, None, "lat", "lon"),
        P(None, None, "lat", "lon"),
        P(),
        P(),
        P(),
        P(),
        P(),
        P(),
    )
    return jax.shard_map(
        per_device,
        mesh=mesh,
        in_specs=placed,
        out_specs=P(None, None, "lat", "lon"),
        check_vma=False,
    )
```

profile of v0, /device:TPU:1, one launch (start us, length us, event | category | flops | bytes accessed | tf_op | source)
XLA Modules:
  0.0 1333.1 jit_solution(13357171241874565079)
XLA Ops:
  6.5 1.5 fusion.120
  13.5 0.7 subtract_multiply_fusion
  14.2 0.8 fusion.125
  15.0 1.5 convolution_bitcast_fusion.5
  16.5 1.4 multiply_reduce_fusion
  18.6 1.4 convert_multiply_fusion.1
  20.0 1.9 convolution_bitcast_fusion.3
  22.1 121.1 %all-gather.1 = f32[128,2,127,8]{2,3,1,0:T(8,128)S(1)} all-gather(f32[4,2,127,8]{2,3,1,0:T(8,128)S(1)} %copy.93), channel_id=3, replica_groups=mesh['lon'=32,'lat'=16] {'lon'}, dimensions={0}, use_global_device_ids=true | all-gather | bytes 1072896 | tf_op jit(solution)/shard_map/all_gather | solution.py:13
  143.2 98.8 %all-gather = f32[128,2,127]{2,1,0:T(2,128)S(1)} all-gather(f32[4,2,127]{2,1,0:T(2,128)S(1)} %copy.91), channel_id=2, replica_groups=mesh['lon'=32,'lat'=16] {'lon'}, dimensions={0}, use_global_device_ids=true | all-gather | bytes 134112 | tf_op jit(solution)/shard_map/all_gather | solution.py:13
  242.6 209.0 %psum.14 = f32[4,2,127,8]{3,0,2,1:T(4,128)S(1)} all-reduce(f32[4,2,127,8]{3,0,2,1:T(4,128)S(1)} %add_select_fusion.1), channel_id=1, replica_groups=mesh['lon'=32,'lat'=16] {'lon'}, use_global_device_ids=true, to_apply=%region_8.9 | all-reduce | flops 8128 | bytes 65024 | tf_op jit(solution)/shard_map/psum | solution.py:27
  451.8 0.8 copy.100
  453.7 0.8 copy.103
  454.6 0.8 copy_select_fusion
  457.5 2.8 convolution_add_fusion.3
  460.3 1.0 copy-done.2
  461.3 1.9 convolution_bitcast_fusion.2
  463.4 106.5 %all-gather.2 = f32[128,2,127,8]{2,3,1,0:T(8,128)S(1)} all-gather(f32[4,2,127,8]{2,3,1,0:T(8,128)S(1)} %copy.105), channel_id=4, replica_groups=mesh['lon'=32,'lat'=16] {'lon'}, dimensions={0}, use_global_device_ids=true | all-gather | bytes 1072896 | tf_op jit(solution)/shard_map/all_gather | solution.py:13
  569.8 43.1 %while.53 = (s32[]{:T(128)}, f32[4,2,127,1]{2,3,1,0:T(1,128)S(1)}, f32[4,2,127,8]{2,3,1,0:T(8,128)S(1)}, s32[]{:T(128)}, f32[32,4,2,127,1]{3,2,1,4,0:T(2,128)}, ...) while((s32[]{:T(128)}, f32[4,2,127,1]{2,3,1,0:T(1,128)S(1)}, ...), condition=%wide.region_10.11_spmd, body=%wide.region_9.10_spmd.sunk | while | flops 17278 | bytes 130207 | solution.py:22
  571.9 0.7 constant_dynamic-slice_fusion.9
  574.7 0.7 constant_dynamic-slice_fusion.9
  578.9 0.7 constant_dynamic-slice_fusion.9
  583.0 0.7 constant_dynamic-slice_fusion.9
  585.8 0.7 constant_dynamic-slice_fusion.9
  587.2 0.7 constant_dynamic-slice_fusion.9
  590.0 0.7 constant_dynamic-slice_fusion.9
  594.2 0.7 constant_dynamic-slice_fusion.9
  596.9 0.7 constant_dynamic-slice_fusion.9
  603.9 0.7 constant_dynamic-slice_fusion.9
  609.4 0.7 constant_dynamic-slice_fusion.9
  612.2 0.7 constant_dynamic-slice_fusion.9
  613.4 205.5 %psum.15 = f32[4,2,127,8]{3,0,2,1:T(4,128)S(1)} all-reduce(f32[4,2,127,8]{3,0,2,1:T(4,128)S(1)} %add_select_fusion), channel_id=1, replica_groups=mesh['lon'=32,'lat'=16] {'lon'}, use_global_device_ids=true, to_apply=%region_11.12 | all-reduce | flops 8128 | bytes 65024 | tf_op jit(solution)/shard_map/psum | solution.py:27
  819.9 1.0 copy.112
  821.0 1.4 fusion.24
  822.5 1.4 fusion.33
  825.3 3.9 convolution_add_fusion.2
  829.3 1.9 convolution_bitcast_fusion.1
  831.2 1.1 copy.122
  832.6 0.8 copy.118
  833.4 146.9 %all-gather.3 = f32[64,2,127]{2,1,0:T(2,128)S(1)} all-gather(f32[4,2,127]{2,1,0:T(2,128)S(1)} %copy.121), channel_id=5, replica_groups=mesh['lon'=32,'lat'=16] {'lat'}, dimensions={0}, use_global_device_ids=true | all-gather | bytes 69088 | tf_op jit(solution)/shard_map/all_gather | solution.py:13
  982.6 121.6 %all-gather.9.cloned.1.call-done = f32[64,2,127,128]{3,1,2,0:T(2,128)} async-done(((f32[4,2,127,128]{3,1,2,0:T(2,128)}), f32[64,2,127,128]{3,1,2,0:T(2,128)}) %all-gather.9.cloned.1.call-update) | async-done | bytes 8323088 | tf_op jit(solution)/shard_map/all_gather | solution.py:13
  1104.2 1.6 while.54
  1104.2 1.1 constant_dynamic-slice_fusion.10
  1105.8 4.0 convolution_add_fusion.1
  1109.8 1.9 convolution_bitcast_fusion
  1111.7 1.1 copy.126
  1114.6 185.2 %all-gather.11.cloned.1.call-done = f32[64,2,127,128]{3,1,2,0:T(2,128)} async-done(((f32[4,2,127,128]{3,1,2,0:T(2,128)}), f32[64,2,127,128]{3,1,2,0:T(2,128)}) %all-gather.11.cloned.1.call-update) | async-done | bytes 8323088 | tf_op jit(solution)/shard_map/all_gather | solution.py:13
  1299.9 20.0 %while.55 = (s32[]{:T(128)}, f32[4,2,127,128]{3,2,1,0:T(8,128)S(1)}, s32[]{:T(128)}, f32[16,4,2,127,1]{3,2,1,4,0:T(2,128)S(1)}, f32[16,4,2,127,128]{4,2,3,1,0:T(...) while((s32[]{:T(128)}, f32[4,2,127,128]{3,2,1,0:T(8,128)S(1)}, s32[]{:T(128)}, ...), condition=%wide.region_15.16_spmd, body=%wide.region_14.15_spmd.sunk | while | flops 260102 | bytes 2613299 | solution.py:22
  1299.9 1.1 constant_dynamic-slice_fusion.11
  1301.3 1.1 constant_dynamic-slice_fusion.11
  1302.8 1.1 constant_dynamic-slice_fusion.11
  1304.2 1.1 constant_dynamic-slice_fusion.11
  1305.6 1.1 constant_dynamic-slice_fusion.11
  1307.0 1.1 constant_dynamic-slice_fusion.11
  1308.4 1.1 constant_dynamic-slice_fusion.11
  1309.8 1.1 constant_dynamic-slice_fusion.11
  1311.2 1.1 constant_dynamic-slice_fusion.11
  1312.6 1.1 constant_dynamic-slice_fusion.11
  1314.0 1.1 constant_dynamic-slice_fusion.11
  1315.4 1.1 constant_dynamic-slice_fusion.11
  1316.8 1.1 constant_dynamic-slice_fusion.11
  1318.2 1.1 constant_dynamic-slice_fusion.11
  1319.9 3.0 convolution_add_fusion
  1322.9 1.8 fusion.38
  1325.1 0.9 fusion.40
  (268 shorter events, 54.5 us)
Async XLA Ops:
  6.5 1316.3 %copy-start = (f32[2,127,127]{2,0,1:T(2,128)S(1)}, f32[2,127,127]{2,0,1:T(2,128)}, u32[]{:S(2)}) copy-start(f32[2,127,127]{2,0,1:T(2,128)} %param.23) | copy-start | bytes 387100
  6.5 13.4 %copy-start.5 = (bf16[2,127,8,128]{3,2,1,0:T(8,128)(2,1)S(1)}, bf16[2,127,8,128]{3,2,1,0:T(8,128)(2,1)}, u32[]{:S(2)}) copy-start(bf16[2,127,8,128]{3,2,1,0:T(8,128)(2,1)} %param.16) | copy-start | bytes 1560580
  6.5 13.4 %copy-start.1 = (bf16[2,127,8,128]{3,2,1,0:T(8,128)(2,1)S(1)}, bf16[2,127,8,128]{3,2,1,0:T(8,128)(2,1)}, u32[]{:S(2)}) copy-start(bf16[2,127,8,128]{3,2,1,0:T(8,128)(2,1)} %param.17) | copy-start | bytes 1560580
  6.5 1097.6 %all-gather.9.cloned.1.call-start = ((), (), s32[]{:S(2)}) async-start(), calls=%async_computation | async-start | bytes 8843264 | tf_op jit(solution)/shard_map/all_gather | solution.py:13
  18.6 1.4 copy-start.7
  143.2 308.4 %copy-start.13 = (f32[4,2,127]{2,1,0:T(2,128)}, f32[4,2,127]{2,1,0:T(2,128)S(1)}, u32[]{:S(2)}) copy-start(f32[4,2,127]{2,1,0:T(2,128)S(1)} %copy.91) | copy-start | bytes 12196
  242.0 0.6 copy-start.6
  451.6 3.0 copy-start.4
  451.7 3.8 copy-start.15
  454.6 2.9 copy-start.12
  455.5 365.5 %copy-start.20 = (pred[40]{0:T(512)(128)(4,1)}, pred[40]{0:T(512)(128)(4,1)S(1)}, u32[]{:S(2)}) copy-start(pred[40]{0:T(512)(128)(4,1)S(1)} %get-tuple-element.377) | copy-start | bytes 124
  455.5 366.9 %copy-start.18 = (pred[40]{0:T(512)(128)(4,1)}, pred[40]{0:T(512)(128)(4,1)S(1)}, u32[]{:S(2)}) copy-start(pred[40]{0:T(512)(128)(4,1)S(1)} %get-tuple-element.376) | copy-start | bytes 124
  455.5 368.4 %copy-start.16 = (pred[40]{0:T(512)(128)(4,1)}, pred[40]{0:T(512)(128)(4,1)S(1)}, u32[]{:S(2)}) copy-start(pred[40]{0:T(512)(128)(4,1)S(1)} %get-tuple-element.375) | copy-start | bytes 124
  455.6 1.8 copy-start.8
  455.6 1.8 copy-start.27
  457.5 3.8 copy-start.26
  460.3 1.0 copy-start.2
  461.3 151.6 %copy-start.14 = (f32[4,2,127]{2,1,0:T(2,128)S(1)}, f32[4,2,127]{2,1,0:T(2,128)}, u32[]{:S(2)}) copy-start(f32[4,2,127]{2,1,0:T(2,128)} %copy-done.13) | copy-start | bytes 12196
  819.9 4.1 copy-start.3
  821.0 3.9 copy-start.22
  821.0 3.9 copy-start.23
  821.0 4.3 copy-start.25
  824.9 4.3 copy-start.24
  825.3 5.9 copy-start.9
  829.3 151.3 %copy-start.21 = (pred[40]{0:T(512)(128)(4,1)S(1)}, pred[40]{0:T(512)(128)(4,1)}, u32[]{:S(2)}) copy-start(pred[40]{0:T(512)(128)(4,1)} %copy-done.20) | copy-start | bytes 124
  831.2 149.8 %copy-start.19 = (pred[40]{0:T(512)(128)(4,1)S(1)}, pred[40]{0:T(512)(128)(4,1)}, u32[]{:S(2)}) copy-start(pred[40]{0:T(512)(128)(4,1)} %copy-done.18) | copy-start | bytes 124
  831.2 150.3 %copy-start.17 = (pred[40]{0:T(512)(128)(4,1)S(1)}, pred[40]{0:T(512)(128)(4,1)}, u32[]{:S(2)}) copy-start(pred[40]{0:T(512)(128)(4,1)} %copy-done.16) | copy-start | bytes 124
  832.3 467.5 %all-gather.11.cloned.1.call-start = ((), (), s32[]{:S(2)}) async-start(), calls=%async_computation.1 | async-start | bytes 8843264 | tf_op jit(solution)/shard_map/all_gather | solution.py:13
  1104.2 1.6 copy-start.10
  1299.9 20.0 %copy-start.11 = (f32[2,127,4]{2,1,0:T(8,128)S(1)}, f32[2,127,4]{2,1,0:T(8,128)}, u32[]{:S(2)}) copy-start(f32[2,127,4]{2,1,0:T(8,128)} %copy.118) | copy-start | bytes 12196
Sparse Core Ops, SparseCore 0:
  832.4 271.6 all-gather.8
  1112.9 186.9 all-gather.10
where the time goes:
time: 1340 us; the launch traced here: 1330 us
  blocking collectives  888 us (66%)
  waiting for transfers between devices  307 us (23%)
  local copies, waits for them, and re-layouts  68.4 us (5%)
  matrix products  35.1 us (3%)
  between operations  17 us (1%)
  other arithmetic  16.9 us (1%)
    all_gather x4, blocking collectives, prefix_2(): gathered = jax.tree.map(lambda a: lax.all_gather(a, axis), part)  473 us
    psum x2, blocking collectives, from_root(): return lax.psum(kept, axis)  415 us
    all_gather x2, waiting for transfers between devices, prefix_2(): gathered = jax.tree.map(lambda a: lax.all_gather(a, axis), part)  307 us
    dynamic_slice x46, local copies, waits for them, and re-layouts, one(): lax.dynamic_index_in_dim(a, source, 0, False)  37.5 us
  transfers between devices with their start and end apart: 2, of which 2 were waited for; matrix products, arithmetic and copies ran while one was open for 0% of the time, Pallas kernels for 0%

commit v1 on v0

v1 whole, which is shorter than its diff:
```python
import functools

import jax
import jax.numpy as jnp
from jax import lax
from jax.experimental import pallas as pl
from jax.experimental.pallas import tpu as pltpu
from jax.sharding import PartitionSpec as P

MOST = 40
KP = 128
MESH = pl.DeviceIdType.MESH
HI = lax.Precision.HIGHEST
AHEAD = 3


def place():
    lon = lax.axis_index("lon")
    lat = lax.axis_index("lat")
    return lon // 8, lon % 8, lat // 4, (lat // 2) % 2, lat % 2


def target(x, z_lo, y, z_hi, core):
    return {"lon": x * 8 + z_lo, "lat": y * 4 + z_hi * 2 + core}


def tables(level_group, lon_reach, lon_weight, lat_reach, lat_weight, rows, cells, nlat, nlon):
    band = lax.axis_index("lat")
    groups = lon_reach.shape[1]
    pick = level_group[None, :] == jnp.arange(groups, dtype=jnp.int32)[:, None]

    def by_level(grouped):
        parts = [jnp.where(pick[g], grouped[:, g][..., None], 0.0) for g in range(groups)]
        return functools.reduce(jnp.add, parts)

    inv_lat = 1.0 / lat_reach
    coef_lat = lat_weight * (1.0 - jnp.exp(-inv_lat))
    row = jnp.arange(rows, dtype=jnp.float32)
    left = (nlat - band * rows).astype(jnp.float32) - row
    both = inv_lat[..., :, None] + inv_lat[..., None, :]
    ratio = jnp.expm1(-both[..., None] * left) / jnp.expm1(-both)[..., None]
    gain = coef_lat[..., None] * jnp.sum(coef_lat[:, :, None, :, None] * ratio, axis=3)
    inv = inv_lat[..., None]
    take_f = jnp.exp(-(rows - 1.0 - row) * inv)
    take_b = jnp.exp(-row * inv) * gain
    take = jnp.stack([take_f, take_b], axis=2)
    give_f = jnp.swapaxes(gain * jnp.exp(-(row + 1.0) * inv), 2, 3)
    give_b = jnp.swapaxes(jnp.exp(-(rows - row) * inv), 2, 3)
    gap = jnp.abs(row[:, None] - row[None, :])
    later = jnp.maximum(row[:, None], row[None, :]).astype(jnp.int32)
    local = jnp.sum(jnp.exp(-gap * inv[..., None]) * gain[..., later], axis=2)

    lanes_j = KP // rows
    take_pat = jnp.tile(jnp.concatenate([take, take], axis=3), (1, 1, 1, 1, lanes_j))
    local_pat = jnp.tile(local, (1, 1, 1, lanes_j))
    give_pat = jnp.concatenate([jnp.tile(give_f, (1, 1, 1, lanes_j)), jnp.tile(give_b, (1, 1, 1, lanes_j))], axis=3)
    apply_pat = jnp.concatenate([local_pat, give_pat], axis=3)
    step_lat = jnp.exp(-rows * inv_lat)
    step_pat = jnp.broadcast_to(jnp.concatenate([step_lat, step_lat], axis=2)[..., None], step_lat.shape[:2] + (8, KP))

    inv_lon = 1.0 / lon_reach
    coef_lon = lon_weight * (1.0 - jnp.exp(-inv_lon))
    pair = inv_lon[..., :, None] + inv_lon[..., None, :]
    amp = coef_lon * jnp.sum(coef_lon[:, :, None, :] / -jnp.expm1(-pair), axis=3)
    cell = jnp.arange(cells, dtype=jnp.float32)
    inv = inv_lon[..., None]
    edge = jnp.concatenate([jnp.exp(-(cells - 1.0 - cell) * inv), jnp.exp(-cell * inv)], axis=2)
    decay = jnp.concatenate([amp[..., None] * jnp.exp(-(cell + 1.0) * inv), amp[..., None] * jnp.exp(-(cells - cell) * inv)], axis=2)
    span = jnp.abs(cell[:, None] - cell[None, :])
    inside = jnp.sum(amp[..., None, None] * jnp.exp(-span * inv[..., None]), axis=2)
    vs = edge.shape[0]
    edge = edge.reshape(vs, groups * 8, cells)
    decay = decay.reshape(vs, groups * 8, cells)

    inv8 = by_level(jnp.concatenate([inv_lon, inv_lon], axis=2))
    closing = 1.0 / -jnp.expm1(-nlon * inv8)
    step_lane = jnp.broadcast_to(by_level(step_lat)[:, :, None, :], (vs, 4, 8, KP))
    take_lane = by_level(take.reshape(vs, groups, 8, rows))
    local_lane = by_level(local)
    give_lane = by_level(jnp.concatenate([give_f, give_b], axis=3))
    return dict(take_pat=take_pat, apply_pat=apply_pat, step_pat=step_pat, edge=edge, decay=decay, inside=inside,
                inv8=inv8, closing=closing, step_lane=step_lane, take_lane=take_lane, local_lane=local_lane, give_lane=give_lane)


def moments_kernel(group_ref, inc_ref, std_ref, row_ref, take_ref, step_ref, edge_ref, m_ref, me_ref, r8_ref, x_ref, bd_ref):
    vs, levels = inc_ref.shape[0], inc_ref.shape[1]
    lane = lax.broadcasted_iota(jnp.int32, (8, KP), 1) // 8
    low = lax.broadcasted_iota(jnp.int32, (8, KP), 0) < 4
    for v in range(vs):
        product = inc_ref[v].astype(jnp.float32) * std_ref[v].astype(jnp.float32)
        x_ref[v, pl.ds(0, levels * 8)] = product.reshape(levels * 8, KP)
        x_ref[v, pl.ds(levels * 8, 8 * (KP - levels))] = jnp.zeros((8 * (KP - levels), KP), jnp.float32)

    def build(t, carry):
        g0, g1 = group_ref[2 * t], group_ref[2 * t + 1]
        block, sub = t // 8, t % 8
        own = jnp.where(low, 2 * sub, 2 * sub + 1) == lane
        for v in range(vs):
            r8_ref[v, block, sub] = jnp.where(low, step_ref[v, g0], step_ref[v, g1])
            for part in range(2):
                tile = jnp.where(own, jnp.where(low, take_ref[v, g0, part], take_ref[v, g1, part]), 0.0)
                bd_ref[v, block, pl.ds(pl.multiple_of(part * 64 + sub * 8, 8), 8)] = tile
        return carry

    lax.fori_loop(0, KP // 2, build, 0)
    for v in range(vs):
        for block in range(8):
            out = jnp.dot(bd_ref[v, block], x_ref[v, pl.ds(block * 128, 128)], precision=HI, preferred_element_type=jnp.float32)
            m_ref[block // 4, v * 4 + block % 4] = out.reshape(2, 8, 8, KP)
        for i in range(8):
            rows = x_ref[v, pl.ds(i, KP, stride=8)]
            sums = lax.dot_general(edge_ref[v], rows, (((1,), (1,)), ((), ())), precision=HI, preferred_element_type=jnp.float32)
            me_ref[v, i] = functools.reduce(jnp.add, [jnp.where(row_ref[...] == g, sums[8 * g:8 * g + 8], 0.0) for g in range(4)])


def exchange_kernel(m_ref, me_ref, r8_ref, step_ref, take_ref, inv_ref, closing_ref,
                    w_ref, wu_ref, u_ref,
                    d1_ref, pm_ref, zr_ref, q_ref, yr_ref, ws_ref,
                    ud1_ref, um_ref, upm_ref, uzr_ref, uq_ref, uyr_ref, uws_ref,
                    ts_ref, tr_ref, xr_ref,
                    d1s, d1r, zss, zrs, yss, yrs, d2s, d2r, ls, lr, xs, xrs):
    x, z_lo, y, z_hi, core = place()
    chunks = m_ref.shape[1]
    mate = target(x, z_lo, y, z_hi, 1 - core)
    across = target(x, z_lo, y, 1 - z_hi, core)
    ys = [target(x, z_lo, (y + d) % 4, z_hi, core) for d in (1, 2, 3)]
    xs_to = [target((x + d) % 4, z_lo, y, z_hi, core) for d in (1, 2, 3)]
    cubes = []
    for m in (1, 2, 4):
        bit = (z_lo // m) % 2
        cubes.append((m, bit, target(x, z_lo + m - 2 * m * bit, y, z_hi, core)))
    partners = [mate, across] + ys + xs_to + [c[2] for c in cubes]
    barrier = pltpu.get_barrier_semaphore()
    for p in partners:
        pl.semaphore_signal(barrier, inc=1, device_id=p, device_id_type=MESH)
    pl.semaphore_wait(barrier, len(partners))

    def remote(src, dst, s, r, to):
        return pltpu.make_async_remote_copy(src_ref=src, dst_ref=dst, send_sem=s, recv_sem=r, device_id=to, device_id_type=MESH)

    def d1(c):
        return remote(m_ref.at[1 - core, c], d1_ref.at[c], d1s.at[c], d1r.at[c], mate)

    def zc(c):
        return remote(pm_ref.at[c], zr_ref.at[c], zss.at[c], zrs.at[c], across)

    def yc(c, d):
        part = (y + d) // 4
        return remote(q_ref.at[c, part], yr_ref.at[c, d - 1], yss.at[c, d - 1], yrs.at[c, d - 1], ys[d - 1])

    def d2(c):
        return remote(ws_ref.at[c], w_ref.at[core, c], d2s.at[c], d2r.at[c], mate)

    last = chunks
    ud1 = remote(um_ref.at[1 - core], ud1_ref, d1s.at[last], d1r.at[last], mate)
    uz = remote(upm_ref, uzr_ref, zss.at[last], zrs.at[last], across)
    uy = [remote(uq_ref.at[(y + d) // 4], uyr_ref.at[d - 1], yss.at[last, d - 1], yrs.at[last, d - 1], ys[d - 1]) for d in (1, 2, 3)]
    ud2 = remote(uws_ref, wu_ref.at[core], d2s.at[last], d2r.at[last], mate)

    def weigh(first, r, own, other):
        a = jnp.where(first, r, 1.0)
        b = jnp.where(first, 1.0, r)
        return a * own[0] + b * other[0], b * own[1] + a * other[1]

    def finish(r8, own, part, zr, slots):
        r16 = r8 * r8
        r32 = r16 * r16
        powers = [jnp.ones_like(r32), r32, r32 * r32]
        wf = jnp.zeros_like(r8)
        wb = jnp.zeros_like(r8)
        for d in (1, 2, 3):
            before = y >= d
            wf = wf + jnp.where(before, powers[d - 1] * slots[d - 1], 0.0)
            wb = wb + jnp.where(before, 0.0, powers[3 - d] * slots[d - 1])
        lower = z_hi == 0
        wf, wb = jnp.where(lower, wf, r16 * wf + zr[0]), jnp.where(lower, r16 * wb + zr[1], wb)
        first = core == 0
        far_f, far_b = r8 * wf, r8 * wb
        mine = jnp.where(first, wf, far_f + part[0]), jnp.where(first, far_b + part[1], wb)
        theirs = jnp.where(first, far_f + own[0], wf), jnp.where(first, wb, far_b + own[1])
        return mine, theirs

    def rate(c):
        return r8_ref[c // 4, core * 4 + c % 4]

    def stage_z(c):
        d1(c).wait_recv()
        f, b = weigh(core == 0, rate(c), (m_ref[core, c, 0], m_ref[core, c, 1]), (d1_ref[c, 0], d1_ref[c, 1]))
        pm_ref[c, 0] = f
        pm_ref[c, 1] = b
        zc(c).start()

    def stage_y(c):
        zc(c).wait_recv()
        r8 = rate(c)
        f, b = weigh(z_hi == 0, r8 * r8, (pm_ref[c, 0], pm_ref[c, 1]), (zr_ref[c, 0], zr_ref[c, 1]))
        q_ref[c, 0] = f
        q_ref[c, 1] = b
        for d in (1, 2, 3):
            yc(c, d).start()

    def stage_w(c):
        for d in (1, 2, 3):
            yc(c, d).wait_recv()
        mine, theirs = finish(rate(c), (m_ref[core, c, 0], m_ref[core, c, 1]), (d1_ref[c, 0], d1_ref[c, 1]),
                              (zr_ref[c, 0], zr_ref[c, 1]), [yr_ref[c, d] for d in range(3)])
        w_ref[core, c, 0] = mine[0]
        w_ref[core, c, 1] = mine[1]
        ws_ref[c, 0] = theirs[0]
        ws_ref[c, 1] = theirs[1]
        d2(c).start()

    def loop(start, stop, body):
        def step(c, carry):
            body(c)
            return carry
        lax.fori_loop(start, stop, step, 0)

    def lon_send(k, to):
        return remote(ts_ref.at[k], tr_ref.at[k], ls.at[k], lr.at[k], to)

    lon0 = remote(me_ref, tr_ref.at[0], ls.at[0], lr.at[0], cubes[0][2])
    lon0.start()
    loop(0, chunks, lambda c: d1(c).start())
    loop(0, AHEAD, stage_z)

    is_f = lax.broadcasted_iota(jnp.int32, (1, 1, 8, KP), 2) < 4
    inv = inv_ref[...][:, None]
    total = me_ref[...]
    prefix = jnp.zeros_like(total)
    copies = [lon0, lon_send(1, cubes[1][2]), lon_send(2, cubes[2][2])]
    for k, (m, bit, to) in enumerate(cubes):
        copies[k].wait_recv()
        other = tr_ref[k]
        upper = bit == 1
        offset = z_lo % m
        gate = jnp.where(is_f == upper, 1.0, 0.0)
        reach = jnp.where(is_f, offset, m - 1 - offset).astype(jnp.float32)
        prefix = prefix + gate * jnp.exp(-128.0 * reach * inv) * other
        whole = jnp.exp(-128.0 * m * inv)
        total = jnp.where(is_f == upper, 1.0, whole) * total + jnp.where(is_f == upper, whole, 1.0) * other
        ts_ref[k + 1] = total
        if k < 2:
            copies[k + 1].start()
        else:
            xcopies = [remote(ts_ref.at[3], xr_ref.at[d], xs.at[d], xrs.at[d], xs_to[d]) for d in range(3)]
            for cp in xcopies:
                cp.start()
        stage_y(k)
        stage_z(k + AHEAD)
    for cp in xcopies:
        cp.wait_recv()
    r1 = jnp.exp(-1024.0 * inv)
    powers = [jnp.ones_like(r1), r1, r1 * r1]
    circle = powers[2] * r1 * total
    for d in range(3):
        circle = circle + jnp.where(is_f, powers[d], powers[2 - d]) * xr_ref[d]
    reach = jnp.where(is_f, z_lo, 7 - z_lo).astype(jnp.float32)
    u_ref[...] = prefix + jnp.exp(-128.0 * reach * inv) * closing_ref[...][:, None] * circle
    for v in range(2):
        for m in range(8):
            acc = take_ref[v, m, 0:1] * u_ref[v, 0]
            for j in range(1, 8):
                acc = acc + take_ref[v, m, j:j + 1] * u_ref[v, j]
            um_ref[v, m // 4, m % 4] = acc
    ud1.start()
    stage_y(3)
    stage_z(6)
    stage_z(7)
    ud1.wait_recv()
    r8u = step_ref[core]
    own_u = (um_ref[core, 0], um_ref[core, 1])
    part_u = (ud1_ref[0], ud1_ref[1])
    f, b = weigh(core == 0, r8u, own_u, part_u)
    upm_ref[0] = f
    upm_ref[1] = b
    uz.start()
    loop(0, 3, stage_w)

    def tail(c, carry):
        stage_y(c)
        stage_w(c - 1)
        return carry

    lax.fori_loop(4, chunks, tail, 0)
    uz.wait_recv()
    zu = (uzr_ref[0], uzr_ref[1])
    f, b = weigh(z_hi == 0, r8u * r8u, (upm_ref[0], upm_ref[1]), zu)
    uq_ref[0] = f
    uq_ref[1] = b
    for cp in uy:
        cp.start()
    stage_w(chunks - 1)
    for cp in uy:
        cp.wait_recv()
    mine, theirs = finish(r8u, own_u, part_u, zu, [uyr_ref[d] for d in range(3)])
    wu_ref[core, 0] = mine[0]
    wu_ref[core, 1] = mine[1]
    uws_ref[0] = theirs[0]
    uws_ref[1] = theirs[1]
    ud2.start()

    def drain(c, carry):
        d1(c).wait_send()
        zc(c).wait_send()
        for d in (1, 2, 3):
            yc(c, d).wait_send()
        d2(c).wait()
        return carry

    lax.fori_loop(0, chunks, drain, 0)
    for cp in copies + xcopies + [ud1, uz] + uy:
        cp.wait_send()
    ud2.wait()


def apply_kernel(group_ref, start_ref, inc_ref, std_ref, row_ref, w_ref, wu_ref, u_ref, inside_ref, decay_ref, apply_ref,
                 local_ref, give_ref, vertical_ref, out_ref, x_ref, bd_ref, z_ref, y_ref, uz_ref):
    vs, levels = inc_ref.shape[0], inc_ref.shape[1]
    lane = lax.broadcasted_iota(jnp.int32, (8, 256), 1)
    lane = jnp.where(lane < 128, lane // 8, (lane % 64) // 4)
    for v in range(vs):
        product = inc_ref[v].astype(jnp.float32) * std_ref[v].astype(jnp.float32)
        x_ref[v, pl.ds(0, levels * 8)] = product.reshape(levels * 8, KP)
        x_ref[v, pl.ds(levels * 8, 8 * (KP - levels))] = jnp.zeros((8 * (KP - levels), KP), jnp.float32)

    def build(k, carry):
        g = group_ref[k]
        own = lane == k % 16
        for v in range(vs):
            bd_ref[v, pl.ds(pl.multiple_of(k * 8, 8), 8)] = jnp.where(own, apply_ref[v, g], 0.0)
        return carry

    lax.fori_loop(0, KP, build, 0)
    for v in range(vs):
        for block in range(8):
            states = w_ref[block // 4, v * 4 + block % 4].reshape(128, KP)
            source = jnp.concatenate([x_ref[v, pl.ds(block * 128, 128)], states], axis=0)
            z_ref[v, pl.ds(block * 128, 128)] = jnp.dot(bd_ref[v, pl.ds(block * 128, 128)], source, precision=HI, preferred_element_type=jnp.float32)
        z_ref[v, pl.ds(8 * KP, 8 * MOST)] = jnp.zeros((8 * MOST, KP), jnp.float32)
        y_ref[v, pl.ds(8 * levels, 8 * (KP - levels))] = jnp.zeros((8 * (KP - levels), KP), jnp.float32)
        for g in range(4):
            window = pl.ds(pl.multiple_of(start_ref[g] * 8, 8), 8 * MOST)
            y_ref[v, window] = jnp.dot(z_ref[v, window], inside_ref[v, g], precision=HI, preferred_element_type=jnp.float32)
        for i in range(8):
            acc = local_ref[v, i, 0:1] * u_ref[v, 0]
            for j in range(1, 8):
                acc = acc + local_ref[v, i, j:j + 1] * u_ref[v, j]
            for m in range(8):
                acc = acc + give_ref[v, i, m:m + 1] * wu_ref[v, m // 4, m % 4]
            for g in range(4):
                uz_ref[pl.ds(8 * g, 8)] = jnp.where(row_ref[...] == g, acc, 0.0)
            carried = lax.dot_general(uz_ref[...], decay_ref[v], (((0,), (0,)), ((), ())), precision=HI, preferred_element_type=jnp.float32)
            filtered = y_ref[v, pl.ds(i, KP, stride=8)] + carried
            x_ref[v, pl.ds(i, KP, stride=8)] = jnp.dot(vertical_ref[v], filtered, precision=HI, preferred_element_type=jnp.float32)
        mixed = x_ref[v, pl.ds(0, levels * 8)].reshape(levels, 8, KP)
        out_ref[v] = (std_ref[v].astype(jnp.float32) * mixed).astype(jnp.bfloat16)


def per_device(nlat, nlon, increment, std_dev, level_group, lon_reach, lon_weight, lat_reach, lat_weight, vertical):
    vs, levels, rows, cells = increment.shape
    f32 = jnp.float32
    groups = jnp.pad(level_group, (0, KP - levels), mode="edge")
    t = tables(groups, lon_reach, lon_weight, lat_reach, lat_weight, rows, cells, nlat, nlon)
    group_row = groups[None, :]
    starts = jnp.sum((level_group[None, :] < jnp.arange(4, dtype=jnp.int32)[:, None]).astype(jnp.int32), axis=1)
    square = jnp.pad(vertical, ((0, 0), (0, KP - levels), (0, KP - levels)))
    vmem = pl.BlockSpec(memory_space=pltpu.VMEM)
    smem = pl.BlockSpec(memory_space=pltpu.SMEM)
    limit = 48 << 20

    m, me, r8 = pl.pallas_call(
        moments_kernel,
        out_shape=(jax.ShapeDtypeStruct((2, 8, 2, 8, 8, KP), f32), jax.ShapeDtypeStruct((vs, 8, 8, KP), f32),
                   jax.ShapeDtypeStruct((vs, 8, 8, 8, KP), f32)),
        in_specs=[smem] + [vmem] * 6,
        out_specs=(vmem,) * 3,
        scratch_shapes=[pltpu.VMEM((vs, 8 * KP, KP), f32), pltpu.VMEM((vs, 8, 128, KP), f32)],
        compiler_params=pltpu.CompilerParams(vmem_limit_bytes=limit),
        name="moments",
    )(groups, increment, std_dev, group_row, t["take_pat"], t["step_pat"], t["edge"])

    dma = pltpu.SemaphoreType.DMA
    chunk = (2, 8, 8, KP)
    small = (2, 4, 8, KP)
    w, wu, u = pl.pallas_call(
        exchange_kernel,
        out_shape=(jax.ShapeDtypeStruct((2, 8) + chunk, f32), jax.ShapeDtypeStruct((vs,) + small, f32),
                   jax.ShapeDtypeStruct((vs, 8, 8, KP), f32)),
        in_specs=[vmem] * 7,
        out_specs=(vmem,) * 3,
        scratch_shapes=[
            pltpu.VMEM((8,) + chunk, f32), pltpu.VMEM((8,) + chunk, f32), pltpu.VMEM((8,) + chunk, f32),
            pltpu.VMEM((8,) + chunk, f32), pltpu.VMEM((8, 3) + chunk[1:], f32), pltpu.VMEM((8,) + chunk, f32),
            pltpu.VMEM(small, f32), pltpu.VMEM((vs,) + small, f32), pltpu.VMEM(small, f32), pltpu.VMEM(small, f32),
            pltpu.VMEM(small, f32), pltpu.VMEM((3,) + small[1:], f32), pltpu.VMEM(small, f32),
            pltpu.VMEM((4, vs, 8, 8, KP), f32), pltpu.VMEM((3, vs, 8, 8, KP), f32), pltpu.VMEM((3, vs, 8, 8, KP), f32),
            dma((9,)), dma((9,)), dma((9,)), dma((9,)), dma((9, 3)), dma((9, 3)), dma((9,)), dma((9,)),
            dma((3,)), dma((3,)), dma((3,)), dma((3,)),
        ],
        compiler_params=pltpu.CompilerParams(collective_id=0, has_side_effects=True, vmem_limit_bytes=limit),
        name="exchange",
    )(m, me, r8, t["step_lane"], t["take_lane"], t["inv8"], t["closing"])

    return pl.pallas_call(
        apply_kernel,
        out_shape=jax.ShapeDtypeStruct(increment.shape, jnp.bfloat16),
        in_specs=[smem, smem] + [vmem] * 12,
        out_specs=vmem,
        scratch_shapes=[pltpu.VMEM((vs, 8 * KP, KP), f32), pltpu.VMEM((vs, 8 * KP, 256), f32), pltpu.VMEM((vs, 8 * (KP + MOST), KP), f32),
                        pltpu.VMEM((vs, 8 * (KP + MOST), KP), f32), pltpu.VMEM((32, KP), f32)],
        compiler_params=pltpu.CompilerParams(vmem_limit_bytes=limit),
        name="apply",
    )(groups, starts, increment, std_dev, group_row, w, wu, u, t["inside"], t["decay"], t["apply_pat"],
      t["local_lane"], t["give_lane"], square)


def solution(mesh):
    placed = (P(None, None, "lat", "lon"),) * 2 + (P(),) * 6

    def whole(increment, *rest):
        nlat, nlon = increment.shape[2:]
        body = functools.partial(per_device, nlat, nlon)
        return jax.shard_map(body, mesh=mesh, in_specs=placed, out_specs=P(None, None, "lat", "lon"), check_vma=False)(increment, *rest)

    return whole
```

time: 1340 us -> 124 us (0.09)
  blocking collectives: 888 us -> 0 us
  waiting for transfers between devices: 307 us -> 0 us
  Pallas kernels: 0 us -> 112 us
  local copies, waits for them, and re-layouts: 68.4 us -> 5.49 us
  matrix products: 35.1 us -> 0 us
  between operations: 17 us -> 0.35 us
    all_gather x4 -> x0, blocking collectives: 473 us -> none  [prefix_2(): gathered = jax.tree.map(lambda a: lax.all_gather(a, axis), part)]
    psum x2 -> x0, blocking collectives: 415 us -> none  [from_root(): return lax.psum(kept, axis)]
    all_gather x2 -> x0, waiting for transfers between devices: 307 us -> none  [prefix_2(): gathered = jax.tree.map(lambda a: lax.all_gather(a, axis), part)]
    pallas_call x0 -> x3, Pallas kernels: none -> 112 us  [the longest x1 99.5 us: per_device(): pl.pallas_call(exchange_kernel, out_shape=(jax.ShapeDtypeStruct((2, 8) +...]
    dynamic_slice x46 -> x0, local copies, waits for them, and re-layouts: 37.5 us -> none  [one(): lax.dynamic_index_in_dim(a, source, 0, False)]
    dot_general x29 -> x0, matrix products: 35.1 us -> none  [the longest x16 9.27 us: grouped_product(): jnp.einsum(pattern, window, blocks[:, group], precision=lax.Precision.HIG...]
    mul x50 -> x1, local copies, waits for them, and re-layouts: 22 us -> 0.13 us  [tables(): give_f = jnp.swapaxes(gain * jnp.exp(-(row + 1.0) * inv), 2, 3)]
  transfers between devices with their start and end apart: 2 -> 0, of which waited for: 2 -> 0; matrix products, arithmetic and copies ran while one was open for 0% -> 0% of each run, Pallas kernels for 0% -> 0%
where the time goes in v1:
time: 124 us
  Pallas kernels  112 us (90%)
  other arithmetic  5.65 us (5%)
  local copies, waits for them, and re-layouts  5.49 us (4%)
    pallas_call x1, Pallas kernels, per_device(): pl.pallas_call(exchange_kernel, out_shape=(jax.ShapeDtypeStruct((2, 8) +...  99.5 us
    pallas_call x1, Pallas kernels, per_device(): pl.pallas_call(apply_kernel, out_shape=jax.ShapeDtypeStruct(increment.sha...  8.23 us
    pallas_call x1, Pallas kernels, per_device(): pl.pallas_call(moments_kernel, out_shape=(jax.ShapeDtypeStruct((2, 8, 2,...  4.47 us

profile of v1, /device:TPU:1, one launch (start us, length us, event | category | flops | bytes accessed | tf_op | source)
XLA Modules:
  0.0 123.7 jit_solution(5424680574194638213)
XLA Ops:
  0.0 0.7 multiply_exponential_fusion.4
  0.7 0.7 subtract_multiply_fusion.1
  1.4 0.1 add_negate_fusion
  1.5 0.0 copy-start.9
  1.5 0.2 multiply_reduce_fusion.2
  1.7 0.1 copy.49
  1.9 0.1 bitcast_multiply_fusion
  2.0 0.0 copy-start.4
  2.0 0.1 fusion.3
  2.1 0.1 multiply_exponential_fusion.3
  2.3 0.1 reshape.196
  2.4 0.2 copy-done.4
  2.6 0.7 gather_fusion
  3.3 0.4 multiply_reduce_fusion.1
  3.7 0.0 copy-start.2
  3.7 0.6 copy-done.2
  4.4 0.3 fusion.9
  4.6 0.2 copy.55
  4.8 0.2 copy.56
  5.0 0.2 copy.57
  5.1 0.2 copy.58
  5.3 0.0 copy-done.9
  5.3 0.6 slice.92
  5.9 0.7 pad_add_fusion.group_ref
  6.7 0.3 select_add_fusion
  7.0 0.0 copy-start.7
  7.0 0.0 copy-start.8
  7.0 0.0 copy-start
  7.0 0.0 copy-start.1
  7.0 0.1 tile.16
  7.1 0.5 tile.17.take_ref
  7.6 0.1 copy-done.7
  7.7 0.0 copy-done.8
  7.7 0.2 fusion.1
  8.0 0.1 exponential_multiply_fusion.1
  8.1 0.1 pad_maximum_fusion.3
  8.2 0.1 broadcast_in_dim.277.step_ref
  8.2 0.7 fusion.11.row_ref
  9.0 0.0 copy-done
  9.0 0.0 copy-done.1
  9.0 4.5 %moments.1 = (f32[2,8,2,8,8,128]{5,4,3,2,1,0:T(8,128)S(1)}, f32[2,8,8,128]{3,2,1,0:T(8,128)S(1)}, f32[2,8,8,8,128]{4,3,2,1,0:T(8,128)S(1)}) custom-call(s32[128]{0:T(128)S(1)} %pad_add_fusion.group_ref, bf16[2,127,8,128]{3,2,1,0:T(8,128)(2,1)S(1)} %copy-done, bf16[2,127,8,128]{3,2,1,0:T(8,128)(2,1)S(1)} %copy-done.1, s32[1,128]{1,0:T(1,128)S(1)} %fusion.11.row_ref, ...), custom_call_target="tpu_custom_call" | custom-call | tf_op jit(solution)/shard_map/moments/pallas_call | solution.py:372
  13.4 0.0 copy-start.3
  13.4 0.1 fusion.7
  13.5 0.1 negate_divide_fusion.1
  13.6 0.1 select_add_fusion.4
  13.7 99.5 %exchange.1 = (f32[2,8,2,8,8,128]{5,4,3,2,1,0:T(8,128)S(1)}, f32[2,2,4,8,128]{4,3,2,1,0:T(8,128)S(1)}, f32[2,8,8,128]{3,2,1,0:T(8,128)S(1)}) custom-call(f32[2,8,2,8,8,128]{5,4,3,2,1,0:T(8,128)S(1)} %get-tuple-element.11.m_ref, f32[2,8,8,128]{3,2,1,0:T(8,128)S(1)} %get-tuple-element.12.me_ref, f32[2,8,8,8,128]{4,3,2,1,0:T(8,128)S(1)} %get-tuple-element.13.r8_ref, ...), custom_call_target="tpu_custom_call" | custom-call | tf_op jit(solution)/shard_map/exchange/pallas_call | solution.py:386
  113.2 0.0 copy-start.5
  113.2 0.0 copy-done.3
  113.2 0.2 copy.50
  113.4 0.3 tile.19
  113.7 0.3 copy-done.5
  114.0 0.1 copy.51
  114.1 0.0 copy-start.6
  114.1 0.1 copy.53
  114.2 0.1 copy.52
  114.4 0.1 copy.54
  114.5 0.1 pad_maximum_fusion.apply_ref
  114.7 0.6 multiply_reduce_fusion.inside_ref
  115.3 0.0 copy-done.6
  115.3 0.1 convert_reduce_fusion.start_ref
  115.4 8.2 %apply.1 = bf16[2,127,8,128]{3,2,1,0:T(8,128)(2,1)} custom-call(s32[128]{0:T(128)S(1)} %pad_add_fusion.group_ref, s32[4]{0:T(128)S(1)} %convert_reduce_fusion.start_ref, bf16[2,127,8,128]{3,2,1,0:T(8,128)(2,1)S(1)} %copy-done, bf16[2,127,8,128]{3,2,1,0:T(8,128)(2,1)S(1)} %copy-done.1, s32[1,128]{1,0:T(1,128)S(1)} %fusion.11.row_ref, ...), custom_call_target="tpu_custom_call" | custom-call | tf_op jit(solution)/shard_map/apply/pallas_call | solution.py:405
  (28 shorter events, 0.4 us)
Async XLA Ops:
  1.5 3.8 %copy-start.9 = (s32[127]{0:T(128)S(1)}, s32[127]{0:T(128)}, u32[]{:S(2)}) copy-start(s32[127]{0:T(128)} %param.10) | copy-start | bytes 1528
  2.0 0.6 copy-start.4
  3.7 0.6 copy-start.2
  7.0 0.7 copy-start.7
  7.0 0.7 copy-start.8
  7.0 1.9 %copy-start = (bf16[2,127,8,128]{3,2,1,0:T(8,128)(2,1)S(1)}, bf16[2,127,8,128]{3,2,1,0:T(8,128)(2,1)}, u32[]{:S(2)}) copy-start(bf16[2,127,8,128]{3,2,1,0:T(8,128)(2,1)} %inc_ref.3) | copy-start | bytes 1560580
  7.0 1.9 %copy-start.1 = (bf16[2,127,8,128]{3,2,1,0:T(8,128)(2,1)S(1)}, bf16[2,127,8,128]{3,2,1,0:T(8,128)(2,1)}, u32[]{:S(2)}) copy-start(bf16[2,127,8,128]{3,2,1,0:T(8,128)(2,1)} %std_ref.3) | copy-start | bytes 1560580
  13.4 99.8 %copy-start.3 = (f32[2,4,8,8]{1,0,3,2:T(2,128)S(1)}, f32[2,4,8,8]{1,0,3,2:T(2,128)}, u32[]{:S(2)}) copy-start(f32[2,4,8,8]{1,0,3,2:T(2,128)} %copy-done.2) | copy-start | bytes 6148
  113.2 0.8 copy-start.5
  114.1 1.1 copy-start.6

commit v2 on v1

v2 whole, which is shorter than its diff:
```python
import functools

import jax
import jax.numpy as jnp
from jax import lax
from jax.experimental import pallas as pl
from jax.experimental.pallas import tpu as pltpu
from jax.sharding import PartitionSpec as P

KP = 128
MESH = pl.DeviceIdType.MESH


def place():
    lon = lax.axis_index("lon")
    lat = lax.axis_index("lat")
    return lon // 8, lon % 8, lat // 4, (lat // 2) % 2, lat % 2


def target(x, z_lo, y, z_hi, core):
    return {"lon": x * 8 + z_lo, "lat": y * 4 + z_hi * 2 + core}


def split(a):
    high = a.astype(jnp.bfloat16)
    return high, (a - high.astype(jnp.float32)).astype(jnp.bfloat16)


def product3(a, b, dims=(((1,), (0,)), ((), ()))):
    ah, al = split(a)
    bh, bl = split(b)
    dot = functools.partial(lax.dot_general, dimension_numbers=dims, preferred_element_type=jnp.float32)
    return dot(ah, bh) + (dot(ah, bl) + dot(al, bh))


def rise(t):
    series = 1.0 / 5040.0
    for c in (-1.0 / 720.0, 1.0 / 120.0, -1.0 / 24.0, 1.0 / 6.0, -0.5, 1.0):
        series = series * t + c
    return jnp.where(t < 0.25, t * series, 1.0 - jnp.exp(-t))


def lanes():
    return lax.broadcasted_iota(jnp.int32, (8, KP), 1)


def subs():
    return lax.broadcasted_iota(jnp.int32, (8, KP), 0)


def grouped(param_ref, kind, v, g):
    inv = 1.0 / param_ref[2 * kind, v, g]
    return inv, param_ref[2 * kind + 1, v, g] * (1.0 - jnp.exp(-inv))


def lat_gain(inv, coef, inv_all, coef_all, left):
    total = 0.0
    for q in range(4):
        both = inv + inv_all[q:q + 1]
        total = total + coef_all[q:q + 1] * (rise(both * left) / rise(both))
    return coef * total


def lat_tables(left_end, param_ref, take_ref, step_ref):
    j = (lanes() % 8).astype(jnp.float32)
    for v in range(2):
        for g in range(4):
            inv, coef = grouped(param_ref, 1, v, g)
            take_ref[v, g, 0] = jnp.exp(-(7.0 - j) * inv)
            take_ref[v, g, 1] = jnp.exp(-j * inv) * lat_gain(inv, coef, inv, coef, left_end - j)
            step_ref[v, g] = jnp.exp(-8.0 * inv)


def lane_tables(left_end, row_ref, param_ref, edge_ref, inv8_ref, closing_ref, lane_step_ref, lane_take_ref, gain_ref, nlon):
    low = subs() < 4
    cell = lanes().astype(jnp.float32)
    row = subs().astype(jnp.float32)
    for v in range(2):
        inv8 = jnp.zeros((8, KP), jnp.float32)
        inv_k = jnp.zeros((8, KP), jnp.float32)
        coef_k = jnp.zeros((8, KP), jnp.float32)
        for g in range(4):
            inv, coef = grouped(param_ref, 1, v, g)
            inv_k = jnp.where(row_ref[...] == g, inv, inv_k)
            coef_k = jnp.where(row_ref[...] == g, coef, coef_k)
            inv, _ = grouped(param_ref, 0, v, g)
            edge_ref[v, 8 * g:8 * g + 8] = jnp.exp(-jnp.where(low, 127.0 - cell, cell) * inv)
            inv8 = jnp.where(row_ref[...] == g, inv, inv8)
        inv8_ref[v] = inv8
        closing_ref[v] = 1.0 / rise(nlon * inv8)
        for p in range(4):
            inv, coef = inv_k[p:p + 1], coef_k[p:p + 1]
            gain = lat_gain(inv, coef, inv_k, coef_k, left_end - row)
            gain_ref[v, p] = gain
            lane_step_ref[v, p] = jnp.broadcast_to(jnp.exp(-8.0 * inv), (8, KP))
            lane_take_ref[v, p] = jnp.exp(-(7.0 - row) * inv)
            lane_take_ref[v, 4 + p] = jnp.exp(-row * inv) * gain
        gain_ref[v, 4] = inv_k


def late_tables(left_end, param_ref, gain_ref, inside_ref, decay_ref, apply_ref, local_ref, give_ref):
    low = subs() < 4
    cell = lanes().astype(jnp.float32)
    row = subs().astype(jnp.float32)
    j = (lanes() % 8).astype(jnp.float32)
    part = lanes() % 4
    for v in range(2):
        for g in range(4):
            inv, coef = grouped(param_ref, 0, v, g)
            amp = 0.0
            for q in range(4):
                amp = amp + coef[q:q + 1] / rise(inv + inv[q:q + 1])
            amp = coef * amp
            decay_ref[v, 8 * g:8 * g + 8] = amp * jnp.exp(-jnp.where(low, cell + 1.0, 128.0 - cell) * inv)
            for tile in range(16):
                gap = jnp.abs(row + 8.0 * tile - cell)
                total = 0.0
                for p in range(4):
                    total = total + amp[p:p + 1] * jnp.exp(-gap * inv[p:p + 1])
                inside_ref[v, 8 * tile:8 * tile + 8, KP * g:KP * g + KP] = total
            inv, coef = grouped(param_ref, 1, v, g)
            total = 0.0
            by_lane, coef_lane = jnp.zeros((8, KP), jnp.float32), jnp.zeros((8, KP), jnp.float32)
            for p in range(4):
                gain = lat_gain(inv[p:p + 1], coef[p:p + 1], inv, coef, left_end - jnp.maximum(row, j))
                total = total + gain * jnp.exp(-jnp.abs(row - j) * inv[p:p + 1])
                by_lane = jnp.where(part == p, inv[p:p + 1], by_lane)
                coef_lane = jnp.where(part == p, coef[p:p + 1], coef_lane)
            apply_ref[v, g, :, 0:KP] = total
            gain = lat_gain(by_lane, coef_lane, inv, coef, left_end - row)
            apply_ref[v, g, :, KP:2 * KP] = jnp.where(lanes() < 64, gain * jnp.exp(-(row + 1.0) * by_lane), jnp.exp(-(8.0 - row) * by_lane))
        inv_k = gain_ref[v, 4]
        for p in range(4):
            give_ref[v, p] = gain_ref[v, p] * jnp.exp(-(row + 1.0) * inv_k[p:p + 1])
            give_ref[v, 4 + p] = jnp.exp(-(8.0 - row) * inv_k[p:p + 1])
        for i in range(8):
            total = 0.0
            for p in range(4):
                gain = jnp.where(row >= i, gain_ref[v, p], gain_ref[v, p, i:i + 1])
                total = total + gain * jnp.exp(-jnp.abs(row - i) * inv_k[p:p + 1])
            local_ref[v, i] = total


def filter_kernel(nlat, nlon, raw_group_ref, raw_row_ref, lon_reach_ref, lon_weight_ref, lat_reach_ref, lat_weight_ref, raw_vertical_ref,
                    inc_ref, std_ref, out_ref, row_ref, param_ref, vertical_ref,
                    w_ref, wu_ref, u_ref, inside_ref, decay_ref, apply_ref, local_ref, give_ref, level_ref, both_ref, y_ref, carry_ref, uz_ref,
                    m_ref, me_ref, r8_ref, x_ref, bd_ref, take_pat_ref, step_pat_ref, edge_ref, inv_ref, closing_ref, step_ref, take_ref, gain_ref,
                    d1_ref, pm_ref, zr_ref, q_ref, yr_ref, ws_ref,
                    ud1_ref, um_ref, upm_ref, uzr_ref, uq_ref, uyr_ref, uws_ref,
                    rows_ref, total_ref, xr_ref, back_ref,
                    d1s, d1r, zss, zrs, yss, yrs, d2s, d2r, ls, lr, xs, xrs, bs, br):
    x, z_lo, y, z_hi, core = place()
    chunks = m_ref.shape[1]
    mate = target(x, z_lo, y, z_hi, 1 - core)
    across = target(x, z_lo, y, 1 - z_hi, core)
    ys = [target(x, z_lo, (y + d) % 4, z_hi, core) for d in (1, 2, 3)]
    xs_to = [target((x + d) % 4, z_lo, y, z_hi, core) for d in (1, 2, 3)]
    others = [target(x, (z_lo + d) % 8, y, z_hi, core) for d in range(1, 8)]
    partners = [mate, across] + ys + xs_to + others
    barrier = pltpu.get_barrier_semaphore()
    for p in partners:
        pl.semaphore_signal(barrier, inc=1, device_id=p, device_id_type=MESH)
    levels = inc_ref.shape[1]
    row_ref[:, 0:levels] = raw_row_ref[...]
    row_ref[:, levels:KP] = jnp.broadcast_to(raw_row_ref[:, levels - 1:levels], (1, KP - levels))
    part = subs() % 4
    for kind, ref in enumerate((lon_reach_ref, lon_weight_ref, lat_reach_ref, lat_weight_ref)):
        for v in range(2):
            for g in range(4):
                tile = jnp.full((8, KP), ref[v, g, 0])
                for p in range(1, 4):
                    tile = jnp.where(part == p, ref[v, g, p], tile)
                param_ref[kind, v, g] = tile

    def group_of(k):
        return raw_group_ref[jnp.minimum(k, levels - 1)]

    left_end = (nlat - 8 * lax.axis_index("lat")).astype(jnp.float32)
    lat_tables(left_end, param_ref, take_pat_ref, step_pat_ref)
    for v in range(2):
        product = inc_ref[v].astype(jnp.float32) * std_ref[v].astype(jnp.float32)
        x_ref[v, pl.ds(0, levels * 8)] = product.reshape(levels * 8, KP)
        x_ref[v, pl.ds(levels * 8, 8 * (KP - levels))] = jnp.zeros((8 * (KP - levels), KP), jnp.float32)

    def build(t, carry):
        g0, g1 = group_of(2 * t), group_of(2 * t + 1)
        block, sub = t // 8, t % 8
        low = subs() < 4
        own = jnp.where(low, 2 * sub, 2 * sub + 1) == lanes() // 8
        for v in range(2):
            r8_ref[v, block, sub] = jnp.where(low, step_pat_ref[v, g0], step_pat_ref[v, g1])
            for part in range(2):
                tile = jnp.where(own, jnp.where(low, take_pat_ref[v, g0, part], take_pat_ref[v, g1, part]), 0.0)
                bd_ref[v, block, pl.ds(pl.multiple_of(part * 64 + sub * 8, 8), 8)] = tile
        return carry

    def moments(c):
        v = c // 4
        for half in range(2):
            block = half * 4 + c % 4
            out = product3(bd_ref[v, block], x_ref[v, pl.ds(block * 128, 128)])
            m_ref[half, c] = out.reshape(2, 8, 8, KP)

    def lon_sums():
        lane_tables(left_end, row_ref, param_ref, edge_ref, inv_ref, closing_ref, step_ref, take_ref, gain_ref, float(nlon))
        for v in range(2):
            for i in range(8):
                sums = product3(edge_ref[v], x_ref[v, pl.ds(i, KP, stride=8)], (((1,), (1,)), ((), ())))
                me_ref[i, v] = functools.reduce(jnp.add, [jnp.where(row_ref[...] == g, sums[8 * g:8 * g + 8], 0.0) for g in range(4)])
    def late():
        late_tables(left_end, param_ref, gain_ref, inside_ref, decay_ref, apply_ref, local_ref, give_ref)

        vertical_ref[...] = jnp.zeros_like(vertical_ref)
        vertical_ref[:, 0:levels, 0:levels] = raw_vertical_ref[...]

        def place_level(k, carry):
            g = group_of(k)
            lane = lax.broadcasted_iota(jnp.int32, (8, 2 * KP), 1)
            own = jnp.where(lane < KP, lane // 8, (lane % 64) // 4) == k % 16
            rows = pl.ds(pl.multiple_of(k * 8, 8), 8)
            level_ref[rows] = jnp.full((8, KP), g, jnp.int32)
            for v in range(2):
                both_ref[v, rows] = jnp.where(own, apply_ref[v, g], 0.0)
            return carry

        lax.fori_loop(0, KP, place_level, 0)

    def stage_f(c):
        v = c // 4
        d2(c).wait_recv()
        for half in range(2):
            block = half * 4 + c % 4
            rows = pl.ds(block * 128, 128)
            source = jnp.concatenate([x_ref[v, rows], w_ref[half, c].reshape(128, KP)], axis=0)
            z = product3(both_ref[v, rows], source)
            wide = product3(z, inside_ref[v])
            result = wide[:, 0:KP]
            for g in range(1, 4):
                result = jnp.where(level_ref[rows] == g, wide[:, KP * g:KP * g + KP], result)
            y_ref[v, rows] = result

    def carried():
        ud2.wait_recv()
        for v in range(2):
            for i in range(8):
                acc = local_ref[v, i, 0:1] * u_ref[0, v]
                for j in range(1, 8):
                    acc = acc + local_ref[v, i, j:j + 1] * u_ref[j, v]
                for m in range(8):
                    acc = acc + give_ref[v, m, i:i + 1] * wu_ref[v, m // 4, m % 4]
                for g in range(4):
                    uz_ref[8 * g:8 * g + 8] = jnp.where(row_ref[...] == g, acc, 0.0)
                carry_ref[v, i] = product3(uz_ref[...], decay_ref[v], (((0,), (0,)), ((), ())))

    def mix(v):
        for i in range(8):
            rows = pl.ds(i, KP, stride=8)
            x_ref[v, rows] = product3(vertical_ref[v], y_ref[v, rows] + carry_ref[v, i])
        mixed = x_ref[v, pl.ds(0, levels * 8)].reshape(levels, 8, KP)
        out_ref[v] = (std_ref[v].astype(jnp.float32) * mixed).astype(jnp.bfloat16)

    lax.fori_loop(0, KP // 2, build, 0)
    moments(0)
    lon_sums()
    moments(1)
    pl.semaphore_wait(barrier, len(partners))

    def remote(src, dst, s, r, to):
        return pltpu.make_async_remote_copy(src_ref=src, dst_ref=dst, send_sem=s, recv_sem=r, device_id=to, device_id_type=MESH)

    def d1(c):
        return remote(m_ref.at[1 - core, c], d1_ref.at[c], d1s.at[c], d1r.at[c], mate)

    def zc(c):
        return remote(pm_ref.at[c], zr_ref.at[c], zss.at[c], zrs.at[c], across)

    def yc(c, d):
        part = (y + d) // 4
        return remote(q_ref.at[c, part], yr_ref.at[c, d - 1], yss.at[c, d - 1], yrs.at[c, d - 1], ys[d - 1])

    def d2(c):
        return remote(ws_ref.at[c], w_ref.at[core, c], d2s.at[c], d2r.at[c], mate)

    last = chunks
    ud1 = remote(um_ref.at[1 - core], ud1_ref, d1s.at[last], d1r.at[last], mate)
    uz = remote(upm_ref, uzr_ref, zss.at[last], zrs.at[last], across)
    uy = [remote(uq_ref.at[(y + d) // 4], uyr_ref.at[d - 1], yss.at[last, d - 1], yrs.at[last, d - 1], ys[d - 1]) for d in (1, 2, 3)]
    ud2 = remote(uws_ref, wu_ref.at[core], d2s.at[last], d2r.at[last], mate)

    def weigh(first, r, own, other):
        a = jnp.where(first, r, 1.0)
        b = jnp.where(first, 1.0, r)
        return a * own[0] + b * other[0], b * own[1] + a * other[1]

    def finish(r8, own, part, zr, slots):
        r16 = r8 * r8
        r32 = r16 * r16
        powers = [jnp.ones_like(r32), r32, r32 * r32]
        wf = jnp.zeros_like(r8)
        wb = jnp.zeros_like(r8)
        for d in (1, 2, 3):
            before = y >= d
            wf = wf + jnp.where(before, powers[d - 1] * slots[d - 1], 0.0)
            wb = wb + jnp.where(before, 0.0, powers[3 - d] * slots[d - 1])
        lower = z_hi == 0
        wf, wb = jnp.where(lower, wf, r16 * wf + zr[0]), jnp.where(lower, r16 * wb + zr[1], wb)
        first = core == 0
        far_f, far_b = r8 * wf, r8 * wb
        mine = jnp.where(first, wf, far_f + part[0]), jnp.where(first, far_b + part[1], wb)
        theirs = jnp.where(first, far_f + own[0], wf), jnp.where(first, wb, far_b + own[1])
        return mine, theirs

    def rate(c):
        return r8_ref[c // 4, core * 4 + c % 4]

    def stage_z(c):
        d1(c).wait_recv()
        f, b = weigh(core == 0, rate(c), (m_ref[core, c, 0], m_ref[core, c, 1]), (d1_ref[c, 0], d1_ref[c, 1]))
        pm_ref[c, 0] = f
        pm_ref[c, 1] = b
        zc(c).start()

    def stage_y(c):
        zc(c).wait_recv()
        r8 = rate(c)
        f, b = weigh(z_hi == 0, r8 * r8, (pm_ref[c, 0], pm_ref[c, 1]), (zr_ref[c, 0], zr_ref[c, 1]))
        q_ref[c, 0] = f
        q_ref[c, 1] = b
        for d in (1, 2, 3):
            yc(c, d).start()

    def stage_w(c):
        for d in (1, 2, 3):
            yc(c, d).wait_recv()
        mine, theirs = finish(rate(c), (m_ref[core, c, 0], m_ref[core, c, 1]), (d1_ref[c, 0], d1_ref[c, 1]),
                              (zr_ref[c, 0], zr_ref[c, 1]), [yr_ref[c, d] for d in range(3)])
        w_ref[core, c, 0] = mine[0]
        w_ref[core, c, 1] = mine[1]
        ws_ref[c, 0] = theirs[0]
        ws_ref[c, 1] = theirs[1]
        d2(c).start()

    is_f = lax.broadcasted_iota(jnp.int32, (1, 8, KP), 1) < 4
    gather = [remote(me_ref.at[(z_lo + d) % 8], rows_ref.at[z_lo], ls.at[d - 1], lr.at[d - 1], others[d - 1]) for d in range(1, 8)]
    spread = [remote(back_ref.at[(z_lo + d) % 8], u_ref.at[z_lo], bs.at[d - 1], br.at[d - 1], others[d - 1]) for d in range(1, 8)]
    xcopies = [remote(total_ref, xr_ref.at[d], xs.at[d], xrs.at[d], xs_to[d]) for d in range(3)]

    def lon_totals():
        rows_ref[z_lo] = me_ref[z_lo]
        for cp in gather:
            cp.wait_recv()
        step = jnp.exp(-128.0 * inv_ref[...])
        total = jnp.zeros_like(step)
        for k in range(8):
            total = step * total + jnp.where(is_f, rows_ref[k], rows_ref[7 - k])
        total_ref[...] = total
        for cp in xcopies:
            cp.start()

    def lon_states():
        for cp in xcopies:
            cp.wait_recv()
        inv = inv_ref[...]
        step = jnp.exp(-128.0 * inv)
        r1 = jnp.exp(-1024.0 * inv)
        powers = [jnp.ones_like(r1), r1, r1 * r1]
        state = powers[2] * r1 * total_ref[...]
        for d in range(3):
            state = state + jnp.where(is_f, powers[d], powers[2 - d]) * xr_ref[d]
        states = [closing_ref[...] * state]
        for k in range(7):
            states.append(step * states[-1] + jnp.where(is_f, rows_ref[k], rows_ref[7 - k]))
        for k in range(8):
            back_ref[k] = jnp.where(is_f, states[k], states[7 - k])
        u_ref[z_lo] = back_ref[z_lo]
        for cp in spread:
            cp.start()

    def lon_moments():
        for cp in spread:
            cp.wait_recv()
        for v in range(2):
            for m in range(8):
                acc = take_ref[v, m, 0:1] * u_ref[0, v]
                for j in range(1, 8):
                    acc = acc + take_ref[v, m, j:j + 1] * u_ref[j, v]
                um_ref[v, m // 4, m % 4] = acc
        ud1.start()

    def small_own():
        return step_ref[core], (um_ref[core, 0], um_ref[core, 1]), (ud1_ref[0], ud1_ref[1])

    def small_z():
        ud1.wait_recv()
        r8, own, part = small_own()
        f, b = weigh(core == 0, r8, own, part)
        upm_ref[0] = f
        upm_ref[1] = b
        uz.start()

    def small_y():
        uz.wait_recv()
        r8 = step_ref[core]
        f, b = weigh(z_hi == 0, r8 * r8, (upm_ref[0], upm_ref[1]), (uzr_ref[0], uzr_ref[1]))
        uq_ref[0] = f
        uq_ref[1] = b
        for cp in uy:
            cp.start()

    def small_w():
        for cp in uy:
            cp.wait_recv()
        r8, own, part = small_own()
        mine, theirs = finish(r8, own, part, (uzr_ref[0], uzr_ref[1]), [uyr_ref[d] for d in range(3)])
        wu_ref[core, 0] = mine[0]
        wu_ref[core, 1] = mine[1]
        uws_ref[0] = theirs[0]
        uws_ref[1] = theirs[1]
        ud2.start()

    def early(c):
        if c > 1:
            moments(c)
        d1(c).start()

    for cp in gather:
        cp.start()
    early(0)
    early(1)
    stage_z(0)
    early(2)
    stage_z(1)
    early(3)
    stage_z(2)
    lon_totals()
    early(4)
    early(5)
    lon_states()
    early(6)
    early(7)
    late()
    stage_y(0)
    stage_z(3)
    stage_y(1)
    stage_z(4)
    stage_w(0)
    stage_f(0)
    stage_y(2)
    stage_z(5)
    stage_w(1)
    stage_y(3)
    stage_z(6)
    stage_w(2)
    stage_f(1)
    lon_moments()
    stage_y(4)
    stage_z(7)
    stage_w(3)
    stage_f(2)
    small_z()
    stage_y(5)
    stage_w(4)
    stage_f(3)
    stage_y(6)
    small_y()
    stage_w(5)
    stage_f(4)
    stage_y(7)
    small_w()
    stage_w(6)
    stage_f(5)
    carried()
    mix(0)
    stage_w(7)
    stage_f(6)
    stage_f(7)
    mix(1)

    def drain(c, carry):
        d1(c).wait_send()
        zc(c).wait_send()
        for d in (1, 2, 3):
            yc(c, d).wait_send()
        d2(c).wait_send()
        return carry

    lax.fori_loop(0, chunks, drain, 0)
    for cp in gather + xcopies + spread + [ud1, uz] + uy:
        cp.wait_send()
    ud2.wait_send()


def per_device(nlat, nlon, increment, std_dev, level_group, lon_reach, lon_weight, lat_reach, lat_weight, vertical):
    vs, levels, rows, cells = increment.shape
    f32 = jnp.float32
    vmem = pl.BlockSpec(memory_space=pltpu.VMEM)
    smem = pl.BlockSpec(memory_space=pltpu.SMEM)
    limit = 48 << 20

    dma = pltpu.SemaphoreType.DMA
    chunk = (2, 8, 8, KP)
    small = (2, 4, 8, KP)

    def scratch(*dims):
        return pltpu.VMEM(dims, f32)

    return pl.pallas_call(
        functools.partial(filter_kernel, nlat, nlon),
        out_shape=jax.ShapeDtypeStruct(increment.shape, jnp.bfloat16),
        in_specs=[smem, vmem] + [smem] * 4 + [vmem] * 3,
        out_specs=vmem,
        scratch_shapes=[
            pltpu.VMEM((1, KP), jnp.int32), scratch(4, vs, 4, 8, KP), scratch(vs, KP, KP),
            scratch(2, 8, *chunk), scratch(vs, *small), scratch(8, vs, 8, KP), scratch(vs, KP, 4 * KP), scratch(vs, 32, KP),
            scratch(vs, 4, 8, 2 * KP), scratch(vs, 8, 8, KP), scratch(vs, 8, 8, KP), pltpu.VMEM((8 * KP, KP), jnp.int32),
            scratch(vs, 8 * KP, 2 * KP), scratch(vs, 8 * KP, KP), scratch(vs, 8, KP, KP), scratch(32, KP),
            scratch(2, 8, *chunk), scratch(8, vs, 8, KP), scratch(vs, 8, 8, 8, KP), scratch(vs, 8 * KP, KP), scratch(vs, 8, 128, KP),
            scratch(vs, 4, 2, 8, KP), scratch(vs, 4, 8, KP), scratch(vs, 32, KP), scratch(vs, 8, KP), scratch(vs, 8, KP), scratch(vs, 4, 8, KP),
            scratch(vs, 8, 8, KP), scratch(vs, 5, 8, KP),
            scratch(8, *chunk), scratch(8, *chunk), scratch(8, *chunk), scratch(8, *chunk), scratch(8, 3, *chunk[1:]), scratch(8, *chunk),
            scratch(*small), scratch(vs, *small), scratch(*small), scratch(*small), scratch(*small), scratch(3, *small[1:]), scratch(*small),
            scratch(8, vs, 8, KP), scratch(vs, 8, KP), scratch(3, vs, 8, KP), scratch(8, vs, 8, KP),
            dma((9,)), dma((9,)), dma((9,)), dma((9,)), dma((9, 3)), dma((9, 3)), dma((9,)), dma((9,)),
            dma((7,)), dma((7,)), dma((3,)), dma((3,)), dma((7,)), dma((7,)),
        ],
        compiler_params=pltpu.CompilerParams(collective_id=0, has_side_effects=True, vmem_limit_bytes=limit),
        name="filter",
    )(level_group, level_group[None, :], lon_reach, lon_weight, lat_reach, lat_weight, vertical, increment, std_dev)


def solution(mesh):
    placed = (P(None, None, "lat", "lon"),) * 2 + (P(),) * 6

    def whole(increment, *rest):
        nlat, nlon = increment.shape[2:]
        body = functools.partial(per_device, nlat, nlon)
        return jax.shard_map(body, mesh=mesh, in_specs=placed, out_specs=P(None, None, "lat", "lon"), check_vma=False)(increment, *rest)

    return whole
```

time: 124 us -> 88.7 us (0.72)
  the two profiles are of different devices: /device:TPU:1 before, /device:TPU:65 now
where the time goes in v2:
time: 88.7 us; the launch traced here: 88.5 us
  Pallas kernels  84.5 us (95%)
  local copies, waits for them, and re-layouts  3.85 us (4%)
    pallas_call x1, Pallas kernels, per_device(): pl.pallas_call(functools.partial(filter_kernel, nlat, nlon), out_shape=ja...  84.5 us
    unnamed x16, local copies, waits for them, and re-layouts  3.85 us

profile of v2, /device:TPU:65, one launch (start us, length us, event | category | flops | bytes accessed | tf_op | source)
XLA Modules:
  0.0 88.5 jit_solution(14518875133927719239)
XLA Ops:
  0.0 0.0 copy-start.2
  0.0 0.0 copy-start.3
  0.0 0.0 copy-start.4
  0.0 0.0 copy-start.5
  0.0 0.0 copy-start.6
  0.0 1.0 %copy.9.raw_vertical_ref = f32[2,127,127]{2,1,0:T(8,128)S(1)} copy(f32[2,127,127]{2,0,1:T(2,128)} %param.15) | data formatting | bytes 258064 | tf_op args[7]
  1.0 0.0 copy-done.2
  1.0 0.0 copy-done.3
  1.0 0.0 copy-done.4
  1.0 0.0 copy-done.5
  1.0 0.0 copy-done.6
  1.0 0.0 copy-start
  1.1 1.0 %copy-done = bf16[2,127,8,128]{3,2,1,0:T(8,128)(2,1)S(1)} copy-done((bf16[2,127,8,128]{3,2,1,0:T(8,128)(2,1)S(1)}, bf16[2,127,8,128]{3,2,1,0:T(8,128)(2,1)}, u32[]{:S(2)}) %copy-start) | copy-done | bytes 520216
  2.1 0.0 copy-start.1
  2.1 1.0 %copy-done.1 = bf16[2,127,8,128]{3,2,1,0:T(8,128)(2,1)S(1)} copy-done((bf16[2,127,8,128]{3,2,1,0:T(8,128)(2,1)S(1)}, bf16[2,127,8,128]{3,2,1,0:T(8,128)(2,1)}, u32[]{:S(2)}) %copy-start.1) | copy-done | bytes 520216
  3.1 84.5 %filter.1 = bf16[2,127,8,128]{3,2,1,0:T(8,128)(2,1)S(1)} custom-call(s32[127]{0:T(128)S(1)} %copy-done.6, s32[1,127]{1,0:T(1,128)S(1)} %bitcast.1, f32[2,4,4]{2,1,0:T(4,128)S(1)} %copy-done.2, f32[2,4,4]{2,1,0:T(4,128)S(1)} %copy-done.3, f32[2,4,4]{2,1,0:T(4,128)S(1)} %copy-done.4, f32[2,4,4]{2,1,0:T(4,128)S(1)} %copy-done.5, ...), custom_call_target="tpu_custom_call" | custom-call | tf_op jit(solution)/shard_map/filter/pallas_call | solution.py:507
  87.7 0.8 copy.11
Async XLA Ops:
  0.0 1.0 %copy-start.2 = (f32[2,4,4]{2,1,0:T(4,128)S(1)}, f32[2,4,4]{2,1,0:T(4,128)}, u32[]{:S(2)}) copy-start(f32[2,4,4]{2,1,0:T(4,128)} %lon_reach_ref.1) | copy-start | bytes 388
  0.0 1.0 %copy-start.3 = (f32[2,4,4]{2,1,0:T(4,128)S(1)}, f32[2,4,4]{2,1,0:T(4,128)}, u32[]{:S(2)}) copy-start(f32[2,4,4]{2,1,0:T(4,128)} %lon_weight_ref.1) | copy-start | bytes 388
  0.0 1.0 %copy-start.4 = (f32[2,4,4]{2,1,0:T(4,128)S(1)}, f32[2,4,4]{2,1,0:T(4,128)}, u32[]{:S(2)}) copy-start(f32[2,4,4]{2,1,0:T(4,128)} %lat_reach_ref.1) | copy-start | bytes 388
  0.0 1.0 %copy-start.5 = (f32[2,4,4]{2,1,0:T(4,128)S(1)}, f32[2,4,4]{2,1,0:T(4,128)}, u32[]{:S(2)}) copy-start(f32[2,4,4]{2,1,0:T(4,128)} %lat_weight_ref.1) | copy-start | bytes 388
  0.0 1.0 %copy-start.6 = (s32[127]{0:T(128)S(1)}, s32[127]{0:T(128)}, u32[]{:S(2)}) copy-start(s32[127]{0:T(128)} %raw_group_ref.1) | copy-start | bytes 1528
  1.0 1.0 %copy-start = (bf16[2,127,8,128]{3,2,1,0:T(8,128)(2,1)S(1)}, bf16[2,127,8,128]{3,2,1,0:T(8,128)(2,1)}, u32[]{:S(2)}) copy-start(bf16[2,127,8,128]{3,2,1,0:T(8,128)(2,1)} %inc_ref.1) | copy-start | bytes 1560580
  2.1 1.0 %copy-start.1 = (bf16[2,127,8,128]{3,2,1,0:T(8,128)(2,1)S(1)}, bf16[2,127,8,128]{3,2,1,0:T(8,128)(2,1)}, u32[]{:S(2)}) copy-start(bf16[2,127,8,128]{3,2,1,0:T(8,128)(2,1)} %std_ref.1) | copy-start | bytes 1560580

commit v3 on v2

--- a/solution.py
+++ b/solution.py
@@ -103,7 +103,7 @@
     cell = lanes().astype(jnp.float32)
     row = subs().astype(jnp.float32)
     j = (lanes() % 8).astype(jnp.float32)
-    part = lanes() % 4
+    part = lanes() % 64 // 16
     for v in range(2):
         for g in range(4):
             inv, coef = grouped(param_ref, 0, v, g)
@@ -147,8 +147,8 @@
                     m_ref, me_ref, r8_ref, x_ref, bd_ref, take_pat_ref, step_pat_ref, edge_ref, inv_ref, closing_ref, step_ref, take_ref, gain_ref,
                     d1_ref, pm_ref, zr_ref, q_ref, yr_ref, ws_ref,
                     ud1_ref, um_ref, upm_ref, uzr_ref, uq_ref, uyr_ref, uws_ref,
-                    rows_ref, total_ref, xr_ref, back_ref,
-                    d1s, d1r, zss, zrs, yss, yrs, d2s, d2r, ls, lr, xs, xrs, bs, br):
+                    rows_ref, total_ref, xr_ref, back_ref, zo_ref, un_ref, fo_ref, fi_ref,
+                    d1s, d1r, zss, zrs, yss, yrs, d2s, d2r, ls, lr, xs, xrs, bs, br, uns, unr, fos, fir):
     x, z_lo, y, z_hi, core = place()
     chunks = m_ref.shape[1]
     mate = target(x, z_lo, y, z_hi, 1 - core)
@@ -182,16 +182,25 @@
         x_ref[v, pl.ds(0, levels * 8)] = product.reshape(levels * 8, KP)
         x_ref[v, pl.ds(levels * 8, 8 * (KP - levels))] = jnp.zeros((8 * (KP - levels), KP), jnp.float32)
 
+    starts = [jnp.sum((row_ref[...] < g).astype(jnp.int32)) for g in (1, 2, 3)]
+
     def build(t, carry):
-        g0, g1 = group_of(2 * t), group_of(2 * t + 1)
-        block, sub = t // 8, t % 8
-        low = subs() < 4
-        own = jnp.where(low, 2 * sub, 2 * sub + 1) == lanes() // 8
+        block, half = t // 2, t % 2
+        level = 8 * t + subs()
+        own = lanes() // 8 == 8 * half + subs()
+
+        def choose(rows):
+            tile = jnp.broadcast_to(rows[0], (8, KP))
+            for g in range(1, 4):
+                tile = jnp.where(level >= starts[g - 1], rows[g], tile)
+            return tile
+
         for v in range(2):
-            r8_ref[v, block, sub] = jnp.where(low, step_pat_ref[v, g0], step_pat_ref[v, g1])
-            for part in range(2):
-                tile = jnp.where(own, jnp.where(low, take_pat_ref[v, g0, part], take_pat_ref[v, g1, part]), 0.0)
-                bd_ref[v, block, pl.ds(pl.multiple_of(part * 64 + sub * 8, 8), 8)] = tile
+            for p in range(4):
+                r8_ref[v, block, 2 * p + half] = choose([step_pat_ref[v, g, p:p + 1] for g in range(4)])
+                for part in range(2):
+                    tile = choose([take_pat_ref[v, g, part, p:p + 1] for g in range(4)])
+                    bd_ref[v, block, pl.ds(pl.multiple_of(part * 64 + p * 16 + half * 8, 8), 8)] = jnp.where(own, tile, 0.0)
         return carry
 
     def moments(c):
@@ -216,7 +225,7 @@
         def place_level(k, carry):
             g = group_of(k)
             lane = lax.broadcasted_iota(jnp.int32, (8, 2 * KP), 1)
-            own = jnp.where(lane < KP, lane // 8, (lane % 64) // 4) == k % 16
+            own = jnp.where(lane < KP, lane // 8, lane % 16) == k % 16
             rows = pl.ds(pl.multiple_of(k * 8, 8), 8)
             level_ref[rows] = jnp.full((8, KP), g, jnp.int32)
             for v in range(2):
@@ -259,7 +268,7 @@
         mixed = x_ref[v, pl.ds(0, levels * 8)].reshape(levels, 8, KP)
         out_ref[v] = (std_ref[v].astype(jnp.float32) * mixed).astype(jnp.bfloat16)
 
-    lax.fori_loop(0, KP // 2, build, 0)
+    lax.fori_loop(0, KP // 8, build, 0)
     moments(0)
     lon_sums()
     moments(1)
@@ -272,7 +281,25 @@
         return remote(m_ref.at[1 - core, c], d1_ref.at[c], d1s.at[c], d1r.at[c], mate)
 
     def zc(c):
-        return remote(pm_ref.at[c], zr_ref.at[c], zss.at[c], zrs.at[c], across)
+        return remote(zo_ref.at[c], zr_ref.at[c], zss.at[c], zrs.at[c], across)
+
+    send_e = jnp.where(z_hi == 0, y, 3 - y)
+    recv_e = jnp.where(z_hi == 1, y, 3 - y)
+    send_hub = target(x, z_lo, 3 * z_hi, z_hi, core)
+    recv_to = [target(x, z_lo, jnp.where(z_hi == 1, e, 3 - e), z_hi, core) for e in (1, 2)]
+
+    def unit_out(c):
+        e = jnp.maximum(send_e, 1)
+        return remote(pm_ref.at[c, 1 - z_hi, pl.ds(6, 2)], un_ref.at[c, e - 1], uns.at[c], unr.at[c, e - 1], send_hub)
+
+    def unit_in(c, k):
+        return remote(pm_ref.at[c, 1 - z_hi, pl.ds(6, 2)], un_ref.at[c, k], uns.at[c], unr.at[c, k], across)
+
+    def fix_out(c, k):
+        return remote(fo_ref.at[c, k], fi_ref.at[c], fos.at[c, k], fir.at[c], recv_to[k])
+
+    def fix_in(c):
+        return remote(fo_ref.at[c, 0], fi_ref.at[c], fos.at[c, 0], fir.at[c], across)
 
     def yc(c, d):
         part = (y + d) // 4
@@ -292,7 +319,7 @@
         b = jnp.where(first, 1.0, r)
         return a * own[0] + b * other[0], b * own[1] + a * other[1]
 
-    def finish(r8, own, part, zr, slots):
+    def finish(r8, own, part, zr, slots, fix=None):
         r16 = r8 * r8
         r32 = r16 * r16
         powers = [jnp.ones_like(r32), r32, r32 * r32]
@@ -302,6 +329,10 @@
             before = y >= d
             wf = wf + jnp.where(before, powers[d - 1] * slots[d - 1], 0.0)
             wb = wb + jnp.where(before, 0.0, powers[3 - d] * slots[d - 1])
+        if fix is not None:
+            whole = jnp.concatenate([jnp.zeros((6, 8, KP), jnp.float32), fix], axis=0)
+            wf = wf + jnp.where(z_hi == 0, whole, 0.0)
+            wb = wb + jnp.where(z_hi == 0, 0.0, whole)
         lower = z_hi == 0
         wf, wb = jnp.where(lower, wf, r16 * wf + zr[0]), jnp.where(lower, r16 * wb + zr[1], wb)
         first = core == 0
@@ -313,27 +344,67 @@
     def rate(c):
         return r8_ref[c // 4, core * 4 + c % 4]
 
-    def stage_z(c):
+    def stage_p(c):
         d1(c).wait_recv()
         f, b = weigh(core == 0, rate(c), (m_ref[core, c, 0], m_ref[core, c, 1]), (d1_ref[c, 0], d1_ref[c, 1]))
         pm_ref[c, 0] = f
         pm_ref[c, 1] = b
+        zo_ref[c, 0:8] = jnp.where(z_hi == 0, f, b)
+        zo_ref[c, 8:14] = jnp.where(z_hi == 0, b, f)[0:6]
+
+        @pl.when(send_e > 0)
+        def _():
+            unit_out(c).start()
+
+    def stage_z(c):
+        @pl.when(send_e == 0)
+        def _():
+            for k in range(3):
+                unit_in(c, k).wait_recv()
+                zo_ref[c, 8 + 2 * k:10 + 2 * k] = un_ref[c, k]
+
         zc(c).start()
+
+    def across_parts(c):
+        kept = zr_ref[c, 0:8]
+        rest = jnp.concatenate([zr_ref[c, 8:14], jnp.zeros((2, 8, KP), jnp.float32)], axis=0)
+        return jnp.where(z_hi == 1, kept, rest), jnp.where(z_hi == 1, rest, kept)
 
     def stage_y(c):
         zc(c).wait_recv()
         r8 = rate(c)
-        f, b = weigh(z_hi == 0, r8 * r8, (pm_ref[c, 0], pm_ref[c, 1]), (zr_ref[c, 0], zr_ref[c, 1]))
+        f, b = weigh(z_hi == 0, r8 * r8, (pm_ref[c, 0], pm_ref[c, 1]), across_parts(c))
         q_ref[c, 0] = f
         q_ref[c, 1] = b
         for d in (1, 2, 3):
             yc(c, d).start()
 
+        @pl.when(recv_e == 0)
+        def _():
+            r32 = r8[6:8] * r8[6:8]
+            r32 = r32 * r32
+            third = zr_ref[c, 12:14]
+            second = zr_ref[c, 10:12] + r32 * third
+            fo_ref[c, 1] = third
+            fo_ref[c, 0] = second
+            fi_ref[c] = zr_ref[c, 8:10] + r32 * second
+            for k in range(2):
+                fix_out(c, k).start()
+
+        @pl.when(recv_e == 3)
+        def _():
+            fi_ref[c] = jnp.zeros((2, 8, KP), jnp.float32)
+
     def stage_w(c):
         for d in (1, 2, 3):
             yc(c, d).wait_recv()
+
+        @pl.when((recv_e == 1) | (recv_e == 2))
+        def _():
+            fix_in(c).wait_recv()
+
         mine, theirs = finish(rate(c), (m_ref[core, c, 0], m_ref[core, c, 1]), (d1_ref[c, 0], d1_ref[c, 1]),
-                              (zr_ref[c, 0], zr_ref[c, 1]), [yr_ref[c, d] for d in range(3)])
+                              across_parts(c), [yr_ref[c, d] for d in range(3)], fi_ref[c])
         w_ref[core, c, 0] = mine[0]
         w_ref[core, c, 1] = mine[1]
         ws_ref[c, 0] = theirs[0]
@@ -427,17 +498,25 @@
         cp.start()
     early(0)
     early(1)
+    stage_p(0)
+    early(2)
+    stage_p(1)
     stage_z(0)
-    early(2)
+    early(3)
+    stage_p(2)
     stage_z(1)
-    early(3)
     stage_z(2)
     lon_totals()
     early(4)
+    stage_p(3)
     early(5)
+    stage_p(4)
     lon_states()
     early(6)
+    stage_p(5)
     early(7)
+    stage_p(6)
+    stage_p(7)
     late()
     stage_y(0)
     stage_z(3)
@@ -481,6 +560,16 @@
         zc(c).wait_send()
         for d in (1, 2, 3):
             yc(c, d).wait_send()
+
+        @pl.when(send_e > 0)
+        def _():
+            unit_out(c).wait_send()
+
+        @pl.when(recv_e == 0)
+        def _():
+            for k in range(2):
+                fix_out(c, k).wait_send()
+
         d2(c).wait_send()
         return carry
 
@@ -517,11 +606,12 @@
             scratch(2, 8, *chunk), scratch(8, vs, 8, KP), scratch(vs, 8, 8, 8, KP), scratch(vs, 8 * KP, KP), scratch(vs, 8, 128, KP),
             scratch(vs, 4, 2, 8, KP), scratch(vs, 4, 8, KP), scratch(vs, 32, KP), scratch(vs, 8, KP), scratch(vs, 8, KP), scratch(vs, 4, 8, KP),
             scratch(vs, 8, 8, KP), scratch(vs, 5, 8, KP),
-            scratch(8, *chunk), scratch(8, *chunk), scratch(8, *chunk), scratch(8, *chunk), scratch(8, 3, *chunk[1:]), scratch(8, *chunk),
+            scratch(8, *chunk), scratch(8, *chunk), scratch(8, 14, 8, KP), scratch(8, *chunk), scratch(8, 3, *chunk[1:]), scratch(8, *chunk),
             scratch(*small), scratch(vs, *small), scratch(*small), scratch(*small), scratch(*small), scratch(3, *small[1:]), scratch(*small),
             scratch(8, vs, 8, KP), scratch(vs, 8, KP), scratch(3, vs, 8, KP), scratch(8, vs, 8, KP),
+            scratch(8, 14, 8, KP), scratch(8, 3, 2, 8, KP), scratch(8, 2, 2, 8, KP), scratch(8, 2, 8, KP),
             dma((9,)), dma((9,)), dma((9,)), dma((9,)), dma((9, 3)), dma((9, 3)), dma((9,)), dma((9,)),
-            dma((7,)), dma((7,)), dma((3,)), dma((3,)), dma((7,)), dma((7,)),
+            dma((7,)), dma((7,)), dma((3,)), dma((3,)), dma((7,)), dma((7,)), dma((8,)), dma((8, 3)), dma((8, 2)), dma((8,)),
         ],
         compiler_params=pltpu.CompilerParams(collective_id=0, has_side_effects=True, vmem_limit_bytes=limit),
         name="filter",

time: 88.7 us -> 87.6 us (0.988)
  the two profiles are of different devices: /device:TPU:65 before, /device:TPU:71 now
where the time goes in v3:
time: 87.6 us; the launch traced here: 87.4 us
  Pallas kernels  83.4 us (95%)
  local copies, waits for them, and re-layouts  3.85 us (4%)
    pallas_call x1, Pallas kernels, per_device(): pl.pallas_call(functools.partial(filter_kernel, nlat, nlon), out_shape=ja...  83.4 us
    unnamed x16, local copies, waits for them, and re-layouts  3.85 us

profile of v3, /device:TPU:71, one launch (start us, length us, event | category | flops | bytes accessed | tf_op | source)
XLA Modules:
  0.0 87.4 jit_solution(10924044571367695141)
XLA Ops:
  0.0 0.0 copy-start.2
  0.0 0.0 copy-start.3
  0.0 0.0 copy-start.4
  0.0 0.0 copy-start.5
  0.0 0.0 copy-start.6
  0.0 1.0 %copy.9.raw_vertical_ref = f32[2,127,127]{2,1,0:T(8,128)S(1)} copy(f32[2,127,127]{2,0,1:T(2,128)} %param.15) | data formatting | bytes 258064 | tf_op args[7]
  1.0 0.0 copy-done.2
  1.0 0.0 copy-done.3
  1.0 0.0 copy-done.4
  1.0 0.0 copy-done.5
  1.0 0.0 copy-done.6
  1.0 0.0 copy-start
  1.1 1.0 %copy-done = bf16[2,127,8,128]{3,2,1,0:T(8,128)(2,1)S(1)} copy-done((bf16[2,127,8,128]{3,2,1,0:T(8,128)(2,1)S(1)}, bf16[2,127,8,128]{3,2,1,0:T(8,128)(2,1)}, u32[]{:S(2)}) %copy-start) | copy-done | bytes 520216
  2.1 0.0 copy-start.1
  2.1 1.0 %copy-done.1 = bf16[2,127,8,128]{3,2,1,0:T(8,128)(2,1)S(1)} copy-done((bf16[2,127,8,128]{3,2,1,0:T(8,128)(2,1)S(1)}, bf16[2,127,8,128]{3,2,1,0:T(8,128)(2,1)}, u32[]{:S(2)}) %copy-start.1) | copy-done | bytes 520216
  3.1 83.4 %filter.1 = bf16[2,127,8,128]{3,2,1,0:T(8,128)(2,1)S(1)} custom-call(s32[127]{0:T(128)S(1)} %copy-done.6, s32[1,127]{1,0:T(1,128)S(1)} %bitcast.1, f32[2,4,4]{2,1,0:T(4,128)S(1)} %copy-done.2, f32[2,4,4]{2,1,0:T(4,128)S(1)} %copy-done.3, f32[2,4,4]{2,1,0:T(4,128)S(1)} %copy-done.4, f32[2,4,4]{2,1,0:T(4,128)S(1)} %copy-done.5, ...), custom_call_target="tpu_custom_call" | custom-call | tf_op jit(solution)/shard_map/filter/pallas_call | solution.py:596
  86.6 0.8 copy.11
Async XLA Ops:
  0.0 1.0 %copy-start.2 = (f32[2,4,4]{2,1,0:T(4,128)S(1)}, f32[2,4,4]{2,1,0:T(4,128)}, u32[]{:S(2)}) copy-start(f32[2,4,4]{2,1,0:T(4,128)} %lon_reach_ref.1) | copy-start | bytes 388
  0.0 1.0 %copy-start.3 = (f32[2,4,4]{2,1,0:T(4,128)S(1)}, f32[2,4,4]{2,1,0:T(4,128)}, u32[]{:S(2)}) copy-start(f32[2,4,4]{2,1,0:T(4,128)} %lon_weight_ref.1) | copy-start | bytes 388
  0.0 1.0 %copy-start.4 = (f32[2,4,4]{2,1,0:T(4,128)S(1)}, f32[2,4,4]{2,1,0:T(4,128)}, u32[]{:S(2)}) copy-start(f32[2,4,4]{2,1,0:T(4,128)} %lat_reach_ref.1) | copy-start | bytes 388
  0.0 1.0 %copy-start.5 = (f32[2,4,4]{2,1,0:T(4,128)S(1)}, f32[2,4,4]{2,1,0:T(4,128)}, u32[]{:S(2)}) copy-start(f32[2,4,4]{2,1,0:T(4,128)} %lat_weight_ref.1) | copy-start | bytes 388
  0.0 1.0 %copy-start.6 = (s32[127]{0:T(128)S(1)}, s32[127]{0:T(128)}, u32[]{:S(2)}) copy-start(s32[127]{0:T(128)} %raw_group_ref.1) | copy-start | bytes 1528
  1.0 1.0 %copy-start = (bf16[2,127,8,128]{3,2,1,0:T(8,128)(2,1)S(1)}, bf16[2,127,8,128]{3,2,1,0:T(8,128)(2,1)}, u32[]{:S(2)}) copy-start(bf16[2,127,8,128]{3,2,1,0:T(8,128)(2,1)} %inc_ref.1) | copy-start | bytes 1560580
  2.1 1.0 %copy-start.1 = (bf16[2,127,8,128]{3,2,1,0:T(8,128)(2,1)S(1)}, bf16[2,127,8,128]{3,2,1,0:T(8,128)(2,1)}, u32[]{:S(2)}) copy-start(bf16[2,127,8,128]{3,2,1,0:T(8,128)(2,1)} %std_ref.1) | copy-start | bytes 1560580

commit v4 on v3

--- a/solution.py
+++ b/solution.py
@@ -61,14 +61,13 @@
     return coef * total
 
 
-def lat_tables(left_end, param_ref, take_ref, step_ref):
+def lat_tables(v, left_end, param_ref, take_ref, step_ref):
     j = (lanes() % 8).astype(jnp.float32)
-    for v in range(2):
-        for g in range(4):
-            inv, coef = grouped(param_ref, 1, v, g)
-            take_ref[v, g, 0] = jnp.exp(-(7.0 - j) * inv)
-            take_ref[v, g, 1] = jnp.exp(-j * inv) * lat_gain(inv, coef, inv, coef, left_end - j)
-            step_ref[v, g] = jnp.exp(-8.0 * inv)
+    for g in range(4):
+        inv, coef = grouped(param_ref, 1, v, g)
+        take_ref[v, g, 0] = jnp.exp(-(7.0 - j) * inv)
+        take_ref[v, g, 1] = jnp.exp(-j * inv) * lat_gain(inv, coef, inv, coef, left_end - j)
+        step_ref[v, g] = jnp.exp(-8.0 * inv)
 
 
 def lane_tables(left_end, row_ref, param_ref, edge_ref, inv8_ref, closing_ref, lane_step_ref, lane_take_ref, gain_ref, nlon):
@@ -141,8 +140,8 @@
             local_ref[v, i] = total
 
 
-def filter_kernel(nlat, nlon, raw_group_ref, raw_row_ref, lon_reach_ref, lon_weight_ref, lat_reach_ref, lat_weight_ref, raw_vertical_ref,
-                    inc_ref, std_ref, out_ref, row_ref, param_ref, vertical_ref,
+def filter_kernel(nlat, nlon, raw_group_ref, raw_row_ref, lon_reach_ref, lon_weight_ref, lat_reach_ref, lat_weight_ref, vertical_hbm,
+                    inc_hbm, std_hbm, out_ref, inc_ref, std_ref, raw_vertical_ref, loads, row_ref, param_ref, vertical_ref,
                     w_ref, wu_ref, u_ref, inside_ref, decay_ref, apply_ref, local_ref, give_ref, level_ref, both_ref, y_ref, carry_ref, uz_ref,
                     m_ref, me_ref, r8_ref, x_ref, bd_ref, take_pat_ref, step_pat_ref, edge_ref, inv_ref, closing_ref, step_ref, take_ref, gain_ref,
                     d1_ref, pm_ref, zr_ref, q_ref, yr_ref, ws_ref,
@@ -160,6 +159,13 @@
     barrier = pltpu.get_barrier_semaphore()
     for p in partners:
         pl.semaphore_signal(barrier, inc=1, device_id=p, device_id_type=MESH)
+    fetch = [(pltpu.make_async_copy(inc_hbm.at[v], inc_ref.at[v], loads.at[2 * v]), pltpu.make_async_copy(std_hbm.at[v], std_ref.at[v], loads.at[2 * v + 1]))
+             for v in range(2)]
+    fetch_vertical = pltpu.make_async_copy(vertical_hbm, raw_vertical_ref, loads.at[4])
+    for pair in fetch:
+        for cp in pair:
+            cp.start()
+    fetch_vertical.start()
     levels = inc_ref.shape[1]
     row_ref[:, 0:levels] = raw_row_ref[...]
     row_ref[:, levels:KP] = jnp.broadcast_to(raw_row_ref[:, levels - 1:levels], (1, KP - levels))
@@ -176,32 +182,35 @@
         return raw_group_ref[jnp.minimum(k, levels - 1)]
 
     left_end = (nlat - 8 * lax.axis_index("lat")).astype(jnp.float32)
-    lat_tables(left_end, param_ref, take_pat_ref, step_pat_ref)
-    for v in range(2):
-        product = inc_ref[v].astype(jnp.float32) * std_ref[v].astype(jnp.float32)
-        x_ref[v, pl.ds(0, levels * 8)] = product.reshape(levels * 8, KP)
-        x_ref[v, pl.ds(levels * 8, 8 * (KP - levels))] = jnp.zeros((8 * (KP - levels), KP), jnp.float32)
-
     starts = [jnp.sum((row_ref[...] < g).astype(jnp.int32)) for g in (1, 2, 3)]
 
-    def build(t, carry):
-        block, half = t // 2, t % 2
-        level = 8 * t + subs()
-        own = lanes() // 8 == 8 * half + subs()
-
-        def choose(rows):
-            tile = jnp.broadcast_to(rows[0], (8, KP))
-            for g in range(1, 4):
-                tile = jnp.where(level >= starts[g - 1], rows[g], tile)
-            return tile
-
-        for v in range(2):
+    def prepare(v):
+        lat_tables(v, left_end, param_ref, take_pat_ref, step_pat_ref)
+
+        def build(t, carry):
+            block, half = t // 2, t % 2
+            level = 8 * t + subs()
+            own = lanes() // 8 == 8 * half + subs()
+
+            def choose(rows):
+                tile = jnp.broadcast_to(rows[0], (8, KP))
+                for g in range(1, 4):
+                    tile = jnp.where(level >= starts[g - 1], rows[g], tile)
+                return tile
+
             for p in range(4):
                 r8_ref[v, block, 2 * p + half] = choose([step_pat_ref[v, g, p:p + 1] for g in range(4)])
                 for part in range(2):
                     tile = choose([take_pat_ref[v, g, part, p:p + 1] for g in range(4)])
                     bd_ref[v, block, pl.ds(pl.multiple_of(part * 64 + p * 16 + half * 8, 8), 8)] = jnp.where(own, tile, 0.0)
-        return carry
+            return carry
+
+        lax.fori_loop(0, KP // 8, build, 0)
+        for cp in fetch[v]:
+            cp.wait()
+        product = inc_ref[v].astype(jnp.float32) * std_ref[v].astype(jnp.float32)
+        x_ref[v, pl.ds(0, levels * 8)] = product.reshape(levels * 8, KP)
+        x_ref[v, pl.ds(levels * 8, 8 * (KP - levels))] = jnp.zeros((8 * (KP - levels), KP), jnp.float32)
 
     def moments(c):
         v = c // 4
@@ -220,7 +229,9 @@
         late_tables(left_end, param_ref, gain_ref, inside_ref, decay_ref, apply_ref, local_ref, give_ref)
 
         vertical_ref[...] = jnp.zeros_like(vertical_ref)
-        vertical_ref[:, 0:levels, 0:levels] = raw_vertical_ref[...]
+        fetch_vertical.wait()
+        for v in range(2):
+            vertical_ref[v, 0:levels, 0:levels] = raw_vertical_ref[:, v, :]
 
         def place_level(k, carry):
             g = group_of(k)
@@ -268,8 +279,9 @@
         mixed = x_ref[v, pl.ds(0, levels * 8)].reshape(levels, 8, KP)
         out_ref[v] = (std_ref[v].astype(jnp.float32) * mixed).astype(jnp.bfloat16)
 
-    lax.fori_loop(0, KP // 8, build, 0)
+    prepare(0)
     moments(0)
+    prepare(1)
     lon_sums()
     moments(1)
     pl.semaphore_wait(barrier, len(partners))
@@ -584,7 +596,7 @@
     f32 = jnp.float32
     vmem = pl.BlockSpec(memory_space=pltpu.VMEM)
     smem = pl.BlockSpec(memory_space=pltpu.SMEM)
-    limit = 48 << 20
+    limit = 63 << 20
 
     dma = pltpu.SemaphoreType.DMA
     chunk = (2, 8, 8, KP)
@@ -596,9 +608,10 @@
     return pl.pallas_call(
         functools.partial(filter_kernel, nlat, nlon),
         out_shape=jax.ShapeDtypeStruct(increment.shape, jnp.bfloat16),
-        in_specs=[smem, vmem] + [smem] * 4 + [vmem] * 3,
+        in_specs=[smem, vmem] + [smem] * 4 + [pl.BlockSpec(memory_space=pltpu.HBM)] * 3,
         out_specs=vmem,
         scratch_shapes=[
+            pltpu.VMEM(increment.shape, jnp.bfloat16), pltpu.VMEM(increment.shape, jnp.bfloat16), scratch(levels, vs, levels), dma((5,)),
             pltpu.VMEM((1, KP), jnp.int32), scratch(4, vs, 4, 8, KP), scratch(vs, KP, KP),
             scratch(2, 8, *chunk), scratch(vs, *small), scratch(8, vs, 8, KP), scratch(vs, KP, 4 * KP), scratch(vs, 32, KP),
             scratch(vs, 4, 8, 2 * KP), scratch(vs, 8, 8, KP), scratch(vs, 8, 8, KP), pltpu.VMEM((8 * KP, KP), jnp.int32),
@@ -615,7 +628,7 @@
         ],
         compiler_params=pltpu.CompilerParams(collective_id=0, has_side_effects=True, vmem_limit_bytes=limit),
         name="filter",
-    )(level_group, level_group[None, :], lon_reach, lon_weight, lat_reach, lat_weight, vertical, increment, std_dev)
+    )(level_group, level_group[None, :], lon_reach, lon_weight, lat_reach, lat_weight, jnp.transpose(vertical, (1, 0, 2)), increment, std_dev)
 
 
 def solution(mesh):

time: 87.6 us -> 84.1 us (0.960)
  the two profiles are of different devices: /device:TPU:71 before, /device:TPU:1 now
where the time goes in v4:
time: 84.1 us; the launch traced here: 83.9 us
  Pallas kernels  82.1 us (98%)
  local copies, waits for them, and re-layouts  1.86 us (2%)
    pallas_call x1, Pallas kernels, per_device(): pl.pallas_call(functools.partial(filter_kernel, nlat, nlon), out_shape=ja...  82.1 us
    unnamed x1, local copies, waits for them, and re-layouts  1.86 us

profile of v4, /device:TPU:1, one launch (start us, length us, event | category | flops | bytes accessed | tf_op | source)
XLA Modules:
  0.0 83.9 jit_solution(3941509668386725326)
XLA Ops:
  0.0 82.1 %filter.1 = bf16[2,127,8,128]{3,2,1,0:T(8,128)(2,1)} custom-call(s32[127]{0:T(128)} %raw_group_ref.1, s32[1,127]{1,0:T(1,128)} %bitcast.3, f32[2,4,4]{2,1,0:T(4,128)} %lon_reach_ref.1, f32[2,4,4]{2,1,0:T(4,128)} %lon_weight_ref.1, f32[2,4,4]{2,1,0:T(4,128)} %lat_reach_ref.1, f32[2,4,4]{2,1,0:T(4,128)} %lat_weight_ref.1, f32[127,2,127]{2,1,0:T(2,128)} %bitcast.2, ...), custom_call_target="tpu_custom_call" | custom-call | tf_op jit(solution)/shard_map/filter/pallas_call | solution.py:608
  82.1 1.9 %copy.10 = bf16[2,127,8,128]{3,2,1,0:T(8,128)(2,1)} copy(bf16[2,127,8,128]{3,2,1,0:T(8,128)(2,1)} %filter.1) | data formatting | bytes 1040384
